TPU v7x, 512 devices: a whole 4x4x16 slice. The times are simulated.
512 devices in a mesh: dp: 64 (over y, z), mp: 8 (over x, core).
Axes of the slice: x: 4, y: 4, z: 16, core: 2. Of those that a mesh axis runs over, the one named last changes fastest.
Arguments:
- train_in: bfloat16 [4096, 64, 16], P('dp'), may hold values from -6 to 6
- train_out_grad: bfloat16 [4096, 64, 1024], P('dp', None, 'mp'), may hold values from -6 to 6
- query_in: bfloat16 [4096, 64, 16], P('dp'), may hold values from -6 to 6
- query_out_grad: bfloat16 [4096, 64, 1024], P('dp', None, 'mp'), may hold values from -6 to 6
- query_owner: int32 [4096, 1], P('dp'), may hold values from 0 to 63; in each aligned block of 64 rows (0 to 63, 64 to 127, ...) at most 2 rows name the same one
- sketch_seed: int32 [1], replicated, may hold values from 0 to 1073741823
Outputs:
- kernel: float32 [4096, 4096], P('mp', 'dp')
- owner_scores: float32 [64, 64, 2, 64], P('dp')
Inputs may be any that keep to these rules, and one draw needn't show every extreme that they name: `query_owner`: within the queries of one device (aligned blocks of 64), one owner is named at most 2 times, a bound that some block reaches in every draw.
All inputs are finite; a program needn't handle non-finite values.
Results may differ from a plain program's by a relative error of at most 0.0041.
Values may be sent and summed in bfloat16 or wider, within the bound.
No kernel may reach another device: no remote copies, remote signals or barrier semaphores. Data moves between devices by JAX's collectives and lax.ppermute only.
A program may use at most 64 MiB of HBM per device.

v0:
```python
import math

import jax
import jax.numpy as jnp
from jax import lax
from jax.sharding import Mesh
from jax.sharding import PartitionSpec as P

VW = 1024
R = 16
K = 8192
L = 64
DP = ("dp_0", "dp_1")


hash_factor = 73244475


def joined_along(parts, dim):
    dims = list(parts.shape[1:])
    dims[dim] *= parts.shape[0]
    return jnp.moveaxis(parts, 0, dim).reshape(dims)


def from_everyone(value, axis):
    copies = jnp.broadcast_to(value, (lax.axis_size(axis), *value.shape))
    return lax.all_to_all(copies, axis, split_axis=0, concat_axis=0, tiled=True)


def collect(value, axis, dim):
    return joined_along(from_everyone(value, axis), dim)


def all_blocks(value, axes, sequence):
    parts = value
    for k in sequence:
        parts = lax.all_gather(parts, axes[k])
    done = sequence[::-1]
    back = [done.index(k) for k in range(len(axes))]
    parts = parts.transpose(*back, *range(len(axes), parts.ndim))
    return parts.reshape(-1, *value.shape)


def gathered_by_axis(value, axes, sequence, dim):
    return joined_along(all_blocks(value, axes, sequence), dim)


def cut_along(value, dim, count):
    before, after = (value.shape[:dim], value.shape[dim + 1 :])
    return jnp.moveaxis(value.reshape(*before, count, -1, *after), dim, 0)


def sent_and_summed(value, axis, dim):
    parts = cut_along(value, dim, lax.axis_size(axis))
    arrived = lax.all_to_all(parts, axis, split_axis=0, concat_axis=0, tiled=True)
    return arrived.sum(axis=0)


def of_everyone(value, axis):
    return from_everyone(value, axis).sum(axis=0)


def sign_table(coords, columns, seed_word):
    mixing = coords[:, None] * K + columns[None, :] ^ seed_word
    for round_index in range(2):
        mixing = mixing * hash_factor
        mixing = mixing ^ lax.shift_right_logical(mixing, jnp.full_like(mixing, 16))
    return (1 - 2 * (mixing & 1)).astype(jnp.bfloat16)


def local_grads(inputs, out_grads):
    return jnp.einsum("ntr,ntj->nrj", inputs, out_grads, preferred_element_type=jnp.float32).astype(
        jnp.bfloat16
    )


def shards(train_in, train_out_grad, query_in, query_out_grad, query_owner, sketch_seed):
    seed_word = sketch_seed[0]
    width_parts = lax.axis_size("mp")
    mp_index = lax.axis_index("mp")
    local_width = train_out_grad.shape[2]
    examples = train_in.shape[0]
    train_grads = local_grads(train_in, train_out_grad)
    query_grads = local_grads(query_in, query_out_grad)
    feature_scale = 1.0 / math.sqrt(L * R * VW)
    block_cols = K // width_parts
    columns = mp_index * block_cols + lax.iota(jnp.int32, block_cols)
    running = jnp.zeros((examples, block_cols), jnp.float32)
    shard_rows = collect(train_grads, "mp", 2)
    first_index = jnp.int32(0)
    span_width = shard_rows.shape[2]
    for rank_index in range(R):
        coords = rank_index * VW + first_index + lax.iota(jnp.int32, span_width)
        running = running + jnp.dot(
            shard_rows[:, rank_index, :],
            sign_table(coords, columns, seed_word),
            preferred_element_type=jnp.float32,
        )
    features = (running * feature_scale).astype(jnp.bfloat16)
    gathered = gathered_by_axis(features, DP, (0, 1), 0)
    gram_block = sent_and_summed(
        lax.dot_general(
            gathered, features, (((1,), (1,)), ((), ())), preferred_element_type=jnp.float32
        ),
        "mp",
        0,
    ) * (1.0 / math.sqrt(K))
    queries = query_grads.shape[0]
    owner_parts = lax.axis_size(DP)
    capacity = 2 * queries // owner_parts
    owners = query_owner[:, 0]
    later_index = lax.broadcasted_iota(jnp.int32, (queries, queries), 0)
    earlier = (owners[:, None] == owners[None, :]) & (
        lax.broadcasted_iota(jnp.int32, (queries, queries), 1) < later_index
    )
    slot_rank = jnp.sum(earlier.astype(jnp.int32), axis=1)
    target = owners * capacity + slot_rank
    placing = (
        lax.broadcasted_iota(jnp.int32, (owner_parts * capacity, queries), 0) == target[None, :]
    ).astype(jnp.bfloat16)
    flat_queries = query_grads.reshape(queries, R * local_width)
    outgoing = jnp.dot(placing, flat_queries, preferred_element_type=jnp.float32).astype(
        jnp.bfloat16
    )
    outgoing = outgoing.reshape(owner_parts, capacity, R * local_width)
    flat_train = train_grads.reshape(examples, R * local_width)
    scores = jnp.einsum(
        "sic,nc->sin",
        lax.all_to_all(outgoing, DP, split_axis=0, concat_axis=0, tiled=True),
        flat_train,
        preferred_element_type=jnp.float32,
    )
    score_scale = 1.0 / (L * math.sqrt(R * VW))
    scores = of_everyone(scores, "mp") * score_scale
    return (gram_block, scores[None])


def solution(mesh):
    finer = Mesh(mesh.devices.reshape(4, 16, mesh.shape["mp"]), ("dp_0", "dp_1", "mp"))
    placed = (
        P(DP, None, None),
        P(DP, None, "mp"),
        P(DP, None, None),
        P(DP, None, "mp"),
        P(DP, None),
        P(),
    )
    return jax.shard_map(
        shards,
        mesh=finer,
        in_specs=placed,
        out_specs=(P("mp", DP), P(DP, None, None, None)),
        check_vma=False,
    )
```

profile of v0, /device:TPU:1, one launch (start us, length us, event | category | flops | bytes accessed | tf_op | source)
XLA Modules:
  0.0 264.2 jit_solution(1019639000569791047)
XLA Ops:
  7.2 1.2 copy-done
  8.4 1.3 convolution_convert_fusion.2
  9.7 1.6 broadcast_in_dim.4
  11.4 10.3 %all-to-all-start = ((bf16[8,64,16,128]{3,2,1,0:T(8,128)(2,1)}), bf16[8,64,16,128]{3,2,1,0:T(8,128)(2,1)S(1)}, u32[]{:S(2)}, u32[]{:S(2)}) async-start(bf16[8,64,16,128]{3,2,1,0:T(8,128)(2,1)} %broadcast_in_dim.4), calls=%async_computation | async-start | bytes 4194304 | tf_op jit(solution)/shard_map/all_to_all | solution.py:27
  22.5 25.4 %all-to-all-done = bf16[8,64,16,128]{3,2,1,0:T(8,128)(2,1)S(1)} async-done(((bf16[8,64,16,128]{3,2,1,0:T(8,128)(2,1)}), bf16[8,64,16,128]{3,2,1,0:T(8,128)(2,1)S(1)}, u32[]{:S(2)}, u32[]{:S(2)}) %all-to-all-start) | async-done | bytes 2097184 | tf_op jit(solution)/shard_map/all_to_all | solution.py:27
  48.2 4.2 %fusion.267 = (bf16[64,1,1024]{2,1,0:T(2,128)(2,1)S(1)}, bf16[64,1,1024]{2,1,0:T(2,128)(2,1)S(1)}, bf16[64,1,1024]{2,1,0:T(2,128)(2,1)S(1)}, bf16[64,1,1024]{2,1...) fusion(bf16[64,16,1024]{2,1,0:T(8,128)(2,1)S(1)} %copy_bitcast_, ...), kind=kLoop, calls=%fused_computation.276 | loop fusion | bytes 4194304 | tf_op jit(solution)/shard_map/slice | solution.py:95
  52.4 2.0 fusion.108
  54.4 2.0 fusion.112
  56.3 2.0 fusion.115
  58.3 2.0 fusion.118
  60.3 2.0 fusion.121
  62.2 2.0 fusion.124
  64.2 2.4 fusion.127
  66.6 2.0 fusion.130
  68.5 2.0 fusion.133
  70.5 2.0 fusion.136
  72.5 2.0 fusion.139
  74.4 2.0 fusion.142
  76.4 2.1 fusion.145
  78.5 2.0 fusion.148
  80.5 2.0 fusion.151
  82.5 2.0 fusion.160
  84.5 10.6 %all-gather = bf16[256,1024]{1,0:T(8,128)(2,1)} all-gather(bf16[64,1024]{1,0:T(8,128)(2,1)S(1)} %fusion.160), channel_id=2, replica_groups=mesh['dp_0'=4,'dp_1'=16,'mp'=8] {'dp_0'}, dimensions={0}, use_global_device_ids=true | all-gather | bytes 655360 | tf_op jit(solution)/shard_map/all_gather | solution.py:37
  97.2 14.0 %all-to-all-start.2 = ((bf16[64,2,2048]{2,1,0:T(2,128)(2,1)}), bf16[64,2,2048]{2,1,0:T(2,128)(2,1)S(1)}, u32[]{:S(2)}, u32[]{:S(2)}) async-start(bf16[64,2,2048]{2,1,0:T(2,128)(2,1)} %reshape.138), calls=%async_computation.2 | async-start | bytes 1048576 | tf_op jit(solution)/shard_map/all_to_all | solution.py:129
  111.3 30.4 %all-to-all-done.2 = bf16[64,2,2048]{2,1,0:T(2,128)(2,1)S(1)} async-done(((bf16[64,2,2048]{2,1,0:T(2,128)(2,1)}), bf16[64,2,2048]{2,1,0:T(2,128)(2,1)S(1)}, u32[]{:S(2)}, u32[]{:S(2)}) %all-to-all-start.2) | async-done | bytes 524320 | tf_op jit(solution)/shard_map/all_to_all | solution.py:129
  143.1 11.8 %all-to-all-start.3 = ((f32[8,1,8192]{2,1,0:T(1,128)}), f32[8,1,8192]{2,1,0:T(1,128)S(1)}, u32[]{:S(2)}, u32[]{:S(2)}) async-start(f32[8,1,8192]{2,1,0:T(1,128)} %reshape.145), calls=%async_computation.3 | async-start | bytes 524288 | tf_op jit(solution)/shard_map/all_to_all | solution.py:27
  154.9 67.1 %all-gather.4.cloned.1.call-done = bf16[64,64,1024]{2,1,0:T(8,128)(2,1)} async-done(((bf16[4,64,1024]{2,1,0:T(8,128)(2,1)}), bf16[64,64,1024]{2,1,0:T(8,128)(2,1)}) %all-gather.4.cloned.1.call-update) | async-done | bytes 8388624 | tf_op jit(solution)/shard_map/all_gather | solution.py:37
  222.1 8.4 %copy.19 = bf16[16,4,64,1024]{3,2,0,1:T(8,128)(2,1)} copy(bf16[16,4,64,1024]{3,2,1,0:T(8,128)(2,1)} %bitcast.98) | data formatting | bytes 16777216 | tf_op jit(solution)/shard_map/all_gather | solution.py:37
  230.5 7.0 %fusion.199 = f32[8,512,64]{1,2,0:T(8,128)} fusion(bf16[8,512,1024]{2,1,0:T(8,128)(2,1)} %bitcast.97, bf16[64,1024]{1,0:T(8,128)(2,1)S(1)} %fusion.160), kind=kOutput, calls=%fused_computation.185 | convolution fusion | flops 536870912 | bytes 9568256 | tf_op jit(solution)/shard_map/dot_general | solution.py:102
  237.5 4.0 %all-to-all-start.1 = ((f32[8,512,64]{1,2,0:T(8,128)}), f32[8,512,64]{1,2,0:T(8,128)S(1)}, u32[]{:S(2)}, u32[]{:S(2)}) async-start(f32[8,512,64]{1,2,0:T(8,128)} %fusion.199), calls=%async_computation.1 | async-start | bytes 2097152 | tf_op jit(solution)/shard_map/all_to_all | solution.py:55
  242.0 1.3 reduce
  244.2 12.3 %all-to-all-done.1 = f32[8,512,64]{1,2,0:T(8,128)S(1)} async-done(((f32[8,512,64]{1,2,0:T(8,128)}), f32[8,512,64]{1,2,0:T(8,128)S(1)}, u32[]{:S(2)}, u32[]{:S(2)}) %all-to-all-start.1) | async-done | bytes 1048608 | tf_op jit(solution)/shard_map/all_to_all | solution.py:55
  (43 shorter events, 6.2 us)
Async XLA Ops:
  7.2 1.2 copy-start
  11.4 36.6 %all-to-all-start = ((bf16[8,64,16,128]{3,2,1,0:T(8,128)(2,1)}), bf16[8,64,16,128]{3,2,1,0:T(8,128)(2,1)S(1)}, u32[]{:S(2)}, u32[]{:S(2)}) async-start(bf16[8,64,16,128]{3,2,1,0:T(8,128)(2,1)} %broadcast_in_dim.4), calls=%async_computation | async-start | bytes 4194304 | tf_op jit(solution)/shard_map/all_to_all | solution.py:27
  21.7 200.4 %all-gather.4.cloned.1.call-start = ((), (), s32[]{:S(2)}) async-start(), calls=%async_computation.4 | async-start | bytes 8912896 | tf_op jit(solution)/shard_map/all_gather | solution.py:37
  82.5 12.7 %copy-start.3 = (s32[64,1]{0,1:T(1,128)S(1)}, s32[64,1]{0,1:T(1,128)}, u32[]{:S(2)}) copy-start(s32[64,1]{0,1:T(1,128)} %param.10) | copy-start | bytes 772
  82.5 12.9 %copy-start.1 = (bf16[64,64,128]{2,1,0:T(8,128)(2,1)S(1)}, bf16[64,64,128]{2,1,0:T(8,128)(2,1)}, u32[]{:S(2)}) copy-start(bf16[64,64,128]{2,1,0:T(8,128)(2,1)} %param.9) | copy-start | bytes 3145732
  82.5 12.9 %copy-start.2 = (bf16[64,64,16]{1,2,0:T(8,128)(2,1)S(1)}, bf16[64,64,16]{1,2,0:T(8,128)(2,1)}, u32[]{:S(2)}) copy-start(bf16[64,64,16]{1,2,0:T(8,128)(2,1)} %param.8) | copy-start | bytes 393220
  97.2 44.5 %all-to-all-start.2 = ((bf16[64,2,2048]{2,1,0:T(2,128)(2,1)}), bf16[64,2,2048]{2,1,0:T(2,128)(2,1)S(1)}, u32[]{:S(2)}, u32[]{:S(2)}) async-start(bf16[64,2,2048]{2,1,0:T(2,128)(2,1)} %reshape.138), calls=%async_computation.2 | async-start | bytes 1048576 | tf_op jit(solution)/shard_map/all_to_all | solution.py:129
  143.1 94.4 %all-to-all-start.3 = ((f32[8,1,8192]{2,1,0:T(1,128)}), f32[8,1,8192]{2,1,0:T(1,128)S(1)}, u32[]{:S(2)}, u32[]{:S(2)}) async-start(f32[8,1,8192]{2,1,0:T(1,128)} %reshape.145), calls=%async_computation.3 | async-start | bytes 524288 | tf_op jit(solution)/shard_map/all_to_all | solution.py:27
  237.5 19.0 %all-to-all-start.1 = ((f32[8,512,64]{1,2,0:T(8,128)}), f32[8,512,64]{1,2,0:T(8,128)S(1)}, u32[]{:S(2)}, u32[]{:S(2)}) async-start(f32[8,512,64]{1,2,0:T(8,128)} %fusion.199), calls=%async_computation.1 | async-start | bytes 2097152 | tf_op jit(solution)/shard_map/all_to_all | solution.py:55
Sparse Core Ops, SparseCore 0:
  95.3 126.7 all-gather.3
where the time goes:
time: 268 us; the launch traced here: 264 us
  waiting for transfers between devices  135 us (50%)
  matrix products  41.4 us (15%)
  starting transfers between devices  40.1 us (15%)
  local copies, waits for them, and re-layouts  19.5 us (7%)
  between operations  15.1 us (6%)
  blocking collectives  10.6 us (4%)
    all_gather x1, waiting for transfers between devices, all_blocks(): parts = lax.all_gather(parts, axes[k])  67.1 us
    dot_general x16, matrix products, shards(): jnp.dot(shard_rows[:, rank_index, :], sign_table(coords, columns, seed_wo...  32 us
    all_to_all x1, waiting for transfers between devices, shards(): lax.all_to_all(outgoing, DP, split_axis=0, concat_axis=0, tiled=True)  30.4 us
    all_to_all x2, waiting for transfers between devices, from_everyone(): return lax.all_to_all(copies, axis, split_axis=0, concat_axis=0, tiled=True)  25.4 us
    all_to_all x2, starting transfers between devices, from_everyone(): return lax.all_to_all(copies, axis, split_axis=0, concat_axis=0, tiled=True)  22.2 us
    all_to_all x1, starting transfers between devices, shards(): lax.all_to_all(outgoing, DP, split_axis=0, concat_axis=0, tiled=True)  14 us
    all_to_all x1, waiting for transfers between devices, sent_and_summed(): lax.all_to_all(parts, axis, split_axis=0, concat_axis=0, tiled=True)  12.3 us
    all_gather x1, blocking collectives, all_blocks(): parts = lax.all_gather(parts, axes[k])  10.6 us
  transfers between devices with their start and end apart: 5, of which 4 were waited for; matrix products, arithmetic and copies ran while one was open for 8% of the time, Pallas kernels for 0%

commit v1 on v0

v1 whole, which is shorter than its diff:
```python
import math

import jax
import jax.numpy as jnp
from jax import lax
from jax.sharding import Mesh
from jax.sharding import PartitionSpec as P

VW = 1024
R = 16
K = 8192
L = 64
DP = ("y", "zh", "zl")
MP = ("x", "c")
Z = ("zh", "zl")

hash_factor = 73244475
sign_factor = ((hash_factor + (1 << 16)) << 15) % (1 << 32)
sign_factor = sign_factor - (1 << 32) if sign_factor >= (1 << 31) else sign_factor


def swap(parts, axes):
    return lax.all_to_all(parts, axes, split_axis=0, concat_axis=0, tiled=True)


def from_everyone(value, axes):
    return swap(jnp.broadcast_to(value, (lax.axis_size(axes), *value.shape)), axes)


def sign_table(coords, columns, seed_word):
    high = ((coords ^ lax.shift_right_logical(seed_word, 13)) << 13) * hash_factor
    low = (columns ^ (seed_word & (K - 1))) * hash_factor
    mixed = high[:, None] + low[None, :]
    mixed = mixed ^ lax.shift_right_logical(mixed, jnp.full_like(mixed, 16))
    mixed = mixed * sign_factor
    return jnp.where(mixed < 0, -1.0, 1.0).astype(jnp.bfloat16)


def local_grads(inputs, out_grads):
    return jnp.einsum("ntr,ntj->nrj", inputs, out_grads, preferred_element_type=jnp.float32).astype(
        jnp.bfloat16
    )


def shards(train_in, train_out_grad, query_in, query_out_grad, query_owner, sketch_seed):
    examples, _, width = train_out_grad.shape
    queries = query_in.shape[0]
    ny, nzh, nzl, nx, nc = (lax.axis_size(a) for a in ("y", "zh", "zl", "x", "c"))
    nz = nzh * nzl
    coords_here = R * width

    train_grads = local_grads(train_in, train_out_grad)
    by_y = from_everyone(train_grads, "y")

    query_grads = local_grads(query_in, query_out_grad)
    owners = query_owner[:, 0]
    later = lax.broadcasted_iota(jnp.int32, (queries, queries), 0)
    earlier = (owners[:, None] == owners[None, :]) & (
        lax.broadcasted_iota(jnp.int32, (queries, queries), 1) < later
    )
    slot = jnp.sum(earlier.astype(jnp.int32), axis=1)
    capacity = 2
    target = ((owners % nz) * ny + owners // nz) * capacity + slot
    placing = (
        lax.broadcasted_iota(jnp.int32, (ny * nz * capacity, queries), 0) == target[None, :]
    ).astype(jnp.bfloat16)
    outgoing = jnp.dot(
        placing, query_grads.reshape(queries, coords_here), preferred_element_type=jnp.float32
    ).astype(jnp.bfloat16)
    arrived = swap(outgoing.reshape(nz, ny * capacity, coords_here), Z)
    arrived = arrived.reshape(nz, ny, capacity, coords_here).swapaxes(0, 1)

    seed_word = sketch_seed[0]
    block_cols = K // ny
    columns = lax.axis_index("y") * block_cols + lax.iota(jnp.int32, block_cols)
    first = lax.axis_index(MP) * width
    coords = (
        lax.broadcasted_iota(jnp.int32, (R, width), 0) * VW
        + lax.broadcasted_iota(jnp.int32, (R, width), 1)
        + first
    ).reshape(-1)
    signs = lax.optimization_barrier(sign_table(coords, columns, seed_word))
    partial = jnp.dot(
        by_y.reshape(ny * examples, coords_here), signs, preferred_element_type=jnp.float32
    )
    partial = partial.astype(jnp.bfloat16).reshape(ny, examples, nc, block_cols // nc)
    partial = partial.transpose(0, 2, 1, 3).reshape(ny * nc, examples, block_cols // nc)
    feature_scale = 1.0 / math.sqrt(L * R * VW)
    features = (swap(partial, MP).astype(jnp.float32).sum(axis=0) * feature_scale).astype(
        jnp.bfloat16
    )

    near = from_everyone(features, "zl")
    rows = from_everyone(features, "zh")
    cols = from_everyone(near, "x")
    depth = features.shape[1]
    gram = jnp.einsum(
        "ymk,ank->yamn",
        cols.reshape(nx, nzl * examples, depth),
        rows.reshape(nc, (nzh // nc) * examples, depth),
        preferred_element_type=jnp.float32,
    )
    gram = swap(gram.reshape(ny * nc, nzl * examples, -1), ("y", "c")).sum(axis=0)
    gram = swap(gram.reshape(nzl, examples, -1), "zl") * (1.0 / math.sqrt(K))
    gram = gram.reshape(nzl, examples, nzh // nc, examples).transpose(2, 0, 3, 1)
    gram = gram.reshape(-1, examples)

    arrived = swap(arrived.reshape(ny, nz * capacity, coords_here), "y")
    scores = jnp.einsum(
        "ic,nc->in",
        arrived.reshape(ny * nz * capacity, coords_here),
        train_grads.reshape(examples, coords_here),
        preferred_element_type=jnp.float32,
    )
    score_scale = 1.0 / (L * math.sqrt(R * VW))
    scores = from_everyone(scores.reshape(-1, 2 * examples), MP).sum(axis=0) * score_scale
    return gram, scores.reshape(1, ny * nz, capacity, examples)


def solution(mesh):
    finer = Mesh(mesh.devices.reshape(4, 4, 4, 4, 2), ("y", "zh", "zl", "x", "c"))
    placed = (
        P(DP, None, None),
        P(DP, None, MP),
        P(DP, None, None),
        P(DP, None, MP),
        P(DP, None),
        P(),
    )
    return jax.shard_map(
        shards,
        mesh=finer,
        in_specs=placed,
        out_specs=(P(MP, DP), P(DP, None, None, None)),
        check_vma=False,
    )
```

time: 268 us -> 234 us (0.87); the launches traced: 264 us -> 233 us
  waiting for transfers between devices: 135 us -> 85.7 us
  blocking collectives: 10.6 us -> 55 us
  matrix products: 41.4 us -> 14.8 us
  starting transfers between devices: 40.1 us -> 53.9 us
  between operations: 15.1 us -> 1.45 us
  other arithmetic: 2.31 us -> 6.97 us
  local copies, waits for them, and re-layouts: 19.5 us -> 15.3 us
    all_gather x1 -> x0, waiting for transfers between devices: 67.1 us -> none  [all_blocks(): parts = lax.all_gather(parts, axes[k])]
    all_to_all x0 -> x2, blocking collectives: none -> 55 us  [swap(): return lax.all_to_all(parts, axes, split_axis=0, concat_axis=0, tiled=True)]
    dot_general x19 -> x4, matrix products: 39.6 us -> 12.1 us  [the longest x1 6.86 us: shards(): jnp.dot(by_y.reshape(ny * examples, coords_here), signs, preferred_elemen...]
    all_to_all x4 -> x8, waiting for transfers between devices: 68 us -> 85.7 us  [swap(): return lax.all_to_all(parts, axes, split_axis=0, concat_axis=0, tiled=True)]
    all_to_all x4 -> x8, starting transfers between devices: 40.1 us -> 53.9 us  [swap(): return lax.all_to_all(parts, axes, split_axis=0, concat_axis=0, tiled=True)]
    all_gather x1 -> x0, blocking collectives: 10.6 us -> none  [all_blocks(): parts = lax.all_gather(parts, axes[k])]
    all_gather x1 -> x0, local copies, waits for them, and re-layouts: 8.4 us -> none  [all_blocks(): parts = lax.all_gather(parts, axes[k])]
    convert_element_type x0 -> x2, other arithmetic: none -> 5.77 us  [the longest x1 5.75 us: sign_table(): return jnp.where(mixed < 0, -1.0, 1.0).astype(jnp.bfloat16)]
  transfers between devices with their start and end apart: 5 -> 8, of which waited for: 4 -> 8; matrix products, arithmetic and copies ran while one was open for 8% -> 8% of each run, Pallas kernels for 0% -> 0%
where the time goes in v1:
time: 234 us; the launch traced here: 233 us
  waiting for transfers between devices  85.7 us (37%)
  blocking collectives  55 us (24%)
  starting transfers between devices  53.9 us (23%)
  local copies, waits for them, and re-layouts  15.3 us (7%)
  matrix products  14.8 us (6%)
  other arithmetic  6.97 us (3%)
    all_to_all x8, waiting for transfers between devices, swap(): return lax.all_to_all(parts, axes, split_axis=0, concat_axis=0, tiled=True)  85.7 us
    all_to_all x2, blocking collectives, swap(): return lax.all_to_all(parts, axes, split_axis=0, concat_axis=0, tiled=True)  55 us
    all_to_all x8, starting transfers between devices, swap(): return lax.all_to_all(parts, axes, split_axis=0, concat_axis=0, tiled=True)  53.9 us
    dot_general x1, matrix products, shards(): jnp.dot(by_y.reshape(ny * examples, coords_here), signs, preferred_elemen...  6.86 us
    convert_element_type x1, other arithmetic, sign_table(): return jnp.where(mixed < 0, -1.0, 1.0).astype(jnp.bfloat16)  5.75 us
  transfers between devices with their start and end apart: 8, of which 8 were waited for; matrix products, arithmetic and copies ran while one was open for 8% of the time, Pallas kernels for 0%

profile of v1, /device:TPU:1, one launch (start us, length us, event | category | flops | bytes accessed | tf_op | source)
XLA Modules:
  0.0 233.0 jit_solution(7659877546288361153)
XLA Ops:
  0.6 1.2 copy-done
  1.9 1.3 convolution_convert_fusion.3
  3.2 1.2 broadcast_in_dim.27
  4.4 5.0 %all-to-all-start = ((bf16[4,64,16,128]{3,2,1,0:T(8,128)(2,1)}), bf16[4,64,16,128]{3,2,1,0:T(8,128)(2,1)S(1)}, u32[]{:S(2)}, u32[]{:S(2)}) async-start(bf16[4,64,16,128]{3,2,1,0:T(8,128)(2,1)} %broadcast_in_dim.27), calls=%async_computation | async-start | bytes 2097152 | tf_op jit(solution)/shard_map/all_to_all | solution.py:23
  10.2 5.8 %select_convert_fusion = bf16[2048,2048]{1,0:T(8,128)(2,1)} fusion(s32[2048]{0:T(1024)S(1)} %xor_multiply_fusion, s32[2048]{0:T(1024)S(1)} %multiply_bitcast_fusion), kind=kLoop, calls=%fused_computation.3 | loop fusion | flops 29360128 | bytes 8404992 | tf_op jit(solution)/shard_map/convert_element_type | solution.py:36
  15.9 3.2 %all-to-all-done = bf16[4,64,16,128]{3,2,1,0:T(8,128)(2,1)S(1)} async-done(((bf16[4,64,16,128]{3,2,1,0:T(8,128)(2,1)}), bf16[4,64,16,128]{3,2,1,0:T(8,128)(2,1)S(1)}, u32[]{:S(2)}, u32[]{:S(2)}) %all-to-all-start) | async-done | bytes 1048608 | tf_op jit(solution)/shard_map/all_to_all | solution.py:23
  19.2 6.9 %convolution_convert_fusion = bf16[256,2048]{1,0:T(8,128)(2,1)} fusion(bf16[2048,2048]{1,0:T(8,128)(2,1)} %select_convert_fusion, bf16[32,8,16,128]{3,2,1,0:T(8,128)(2,1)S(1)} %bitcast.56), kind=kOutput, calls=%fused_computation.4 | convolution fusion | flops 2148007936 | bytes 10485760 | tf_op jit(solution)/shard_map/dot_general | solution.py:83
  26.0 1.8 reshape.154
  27.9 1.2 copy.25
  29.1 10.6 %all-to-all-start.1 = ((bf16[8,64,1024]{2,1,0:T(8,128)(2,1)}), bf16[8,64,1024]{2,1,0:T(8,128)(2,1)S(1)}, u32[]{:S(2)}, u32[]{:S(2)}) async-start(bf16[8,64,1024]{2,1,0:T(8,128)(2,1)} %bitcast.4), calls=%async_computation.1 | async-start | bytes 2097152 | tf_op jit(solution)/shard_map/all_to_all | solution.py:23
  39.9 1.3 convolution_convert_fusion.2
  41.2 1.1 fusion.2
  42.4 12.3 %all-to-all-done.1 = bf16[8,64,1024]{2,1,0:T(8,128)(2,1)S(1)} async-done(((bf16[8,64,1024]{2,1,0:T(8,128)(2,1)}), bf16[8,64,1024]{2,1,0:T(8,128)(2,1)S(1)}, u32[]{:S(2)}, u32[]{:S(2)}) %all-to-all-start.1) | async-done | bytes 1048608 | tf_op jit(solution)/shard_map/all_to_all | solution.py:23
  54.7 14.9 %all-to-all-start.7 = ((bf16[16,8,2048]{2,1,0:T(8,128)(2,1)}), bf16[16,8,2048]{2,1,0:T(8,128)(2,1)S(1)}, u32[]{:S(2)}, u32[]{:S(2)}) async-start(bf16[16,8,2048]{2,1,0:T(8,128)(2,1)} %fusion.2), calls=%async_computation.7 | async-start | bytes 1048576 | tf_op jit(solution)/shard_map/all_to_all | solution.py:23
  69.8 22.9 %all-to-all-done.7 = bf16[16,8,2048]{2,1,0:T(8,128)(2,1)S(1)} async-done(((bf16[16,8,2048]{2,1,0:T(8,128)(2,1)}), bf16[16,8,2048]{2,1,0:T(8,128)(2,1)S(1)}, u32[]{:S(2)}, u32[]{:S(2)}) %all-to-all-start.7) | async-done | bytes 524320 | tf_op jit(solution)/shard_map/all_to_all | solution.py:23
  92.7 16.8 %all_to_all.50 = bf16[4,64,1024]{2,1,0:T(8,128)(2,1)S(1)} all-to-all(bf16[4,64,1024]{2,1,0:T(8,128)(2,1)S(1)} %broadcast_in_dim.31), channel_id=1, replica_groups=mesh['y'=4,'zh'=4,'zl'=4,'x'=4,'c'=2] {'zl'}, dimensions={0} | all-to-all | bytes 1048576 | tf_op jit(solution)/shard_map/all_to_all | solution.py:23
  109.5 38.2 %all_to_all.51 = bf16[4,64,1024]{2,1,0:T(8,128)(2,1)} all-to-all(bf16[4,64,1024]{2,1,0:T(8,128)(2,1)S(1)} %broadcast_in_dim.31), channel_id=1, replica_groups=mesh['y'=4,'zh'=4,'zl'=4,'x'=4,'c'=2] {'zh'}, dimensions={0} | all-to-all | bytes 1048576 | tf_op jit(solution)/shard_map/all_to_all | solution.py:23
  147.7 1.6 broadcast_in_dim.32
  149.4 3.6 %all-to-all-start.4 = ((bf16[4,4,64,1024]{3,2,1,0:T(8,128)(2,1)}), bf16[4,4,64,1024]{3,2,1,0:T(8,128)(2,1)S(1)}, u32[]{:S(2)}, u32[]{:S(2)}) async-start(bf16[4,4,64,1024]{3,2,1,0:T(8,128)(2,1)} %broadcast_in_dim.32), calls=%async_computation.4 | async-start | bytes 4194304 | tf_op jit(solution)/shard_map/all_to_all | solution.py:23
  153.0 1.3 copy.28
  155.8 22.1 %all-to-all-done.4 = bf16[4,4,64,1024]{3,2,1,0:T(8,128)(2,1)S(1)} async-done(((bf16[4,4,64,1024]{3,2,1,0:T(8,128)(2,1)}), bf16[4,4,64,1024]{3,2,1,0:T(8,128)(2,1)S(1)}, u32[]{:S(2)}, u32[]{:S(2)}) %all-to-all-start.4) | async-done | bytes 2097184 | tf_op jit(solution)/shard_map/all_to_all | solution.py:23
  177.9 4.1 %all-to-all-start.8 = ((bf16[4,32,2048]{2,1,0:T(8,128)(2,1)}), bf16[4,32,2048]{2,1,0:T(8,128)(2,1)}, u32[]{:S(2)}, u32[]{:S(2)}) async-start(bf16[4,32,2048]{2,1,0:T(8,128)(2,1)} %copy.30), calls=%async_computation.8 | async-start | bytes 1048576 | tf_op jit(solution)/shard_map/all_to_all | solution.py:23
  182.1 2.8 %convolution_bitcast_fusion = f32[4,2,256,128]{2,3,0,1:T(8,128)} fusion(bf16[2,128,1024,1]{2,1,3,0:T(8,128)(2,1)} %bitcast.53, bf16[4,256,1024,1]{2,1,0,3:T(8,128)(2,1)S(1)} %bitcast.52), kind=kOutput, calls=%fused_computation.8 | convolution fusion | flops 536870912 | bytes 3670016 | tf_op jit(solution)/shard_map/ymk,ank->yamn/dot_general | solution.py:97
  184.9 2.5 %copy.26 = f32[4,2,256,128]{3,2,1,0:T(8,128)} copy(f32[4,2,256,128]{2,3,0,1:T(8,128)} %convolution_bitcast_fusion) | data formatting | bytes 2097152 | tf_op jit(solution)/shard_map/ymk,ank->yamn/transpose | solution.py:97
  187.4 1.7 all-to-all-done.8
  189.1 6.9 %all-to-all-start.5 = ((f32[8,256,128]{2,1,0:T(8,128)}), f32[8,256,128]{2,1,0:T(8,128)S(1)}, u32[]{:S(2)}, u32[]{:S(2)}) async-start(f32[8,256,128]{2,1,0:T(8,128)} %bitcast.11), calls=%async_computation.5 | async-start | bytes 2097152 | tf_op jit(solution)/shard_map/all_to_all | solution.py:23
  196.0 1.3 fusion.5
  197.4 13.6 %all-to-all-done.5 = f32[8,256,128]{2,1,0:T(8,128)S(1)} async-done(((f32[8,256,128]{2,1,0:T(8,128)}), f32[8,256,128]{2,1,0:T(8,128)S(1)}, u32[]{:S(2)}, u32[]{:S(2)}) %all-to-all-start.5) | async-done | bytes 1048608 | tf_op jit(solution)/shard_map/all_to_all | solution.py:23
  211.7 4.3 %all-to-all-start.9 = ((f32[8,64,128]{2,1,0:T(8,128)}), f32[8,64,128]{2,1,0:T(8,128)S(1)}, u32[]{:S(2)}, u32[]{:S(2)}) async-start(f32[8,64,128]{2,1,0:T(8,128)} %broadcast_in_dim.33), calls=%async_computation.9 | async-start | bytes 524288 | tf_op jit(solution)/shard_map/all_to_all | solution.py:23
  216.7 5.8 %all-to-all-done.9 = f32[8,64,128]{2,1,0:T(8,128)S(1)} async-done(((f32[8,64,128]{2,1,0:T(8,128)}), f32[8,64,128]{2,1,0:T(8,128)S(1)}, u32[]{:S(2)}, u32[]{:S(2)}) %all-to-all-start.9) | async-done | bytes 262176 | tf_op jit(solution)/shard_map/all_to_all | solution.py:23
  222.5 4.4 %all-to-all-start.6 = ((f32[4,64,128]{2,1,0:T(8,128)}), f32[4,64,128]{2,1,0:T(8,128)S(1)}, u32[]{:S(2)}, u32[]{:S(2)}) async-start(f32[4,64,128]{2,1,0:T(8,128)} %bitcast.12), calls=%async_computation.6 | async-start | bytes 262144 | tf_op jit(solution)/shard_map/all_to_all | solution.py:23
  227.7 4.1 %all-to-all-done.6 = f32[4,64,128]{2,1,0:T(8,128)S(1)} async-done(((f32[4,64,128]{2,1,0:T(8,128)}), f32[4,64,128]{2,1,0:T(8,128)S(1)}, u32[]{:S(2)}, u32[]{:S(2)}) %all-to-all-start.6) | async-done | bytes 131104 | tf_op jit(solution)/shard_map/all_to_all | solution.py:23
  (27 shorter events, 5.5 us)
Async XLA Ops:
  0.6 1.2 copy-start
  4.4 14.8 %all-to-all-start = ((bf16[4,64,16,128]{3,2,1,0:T(8,128)(2,1)}), bf16[4,64,16,128]{3,2,1,0:T(8,128)(2,1)S(1)}, u32[]{:S(2)}, u32[]{:S(2)}) async-start(bf16[4,64,16,128]{3,2,1,0:T(8,128)(2,1)} %broadcast_in_dim.27), calls=%async_computation | async-start | bytes 2097152 | tf_op jit(solution)/shard_map/all_to_all | solution.py:23
  19.2 20.5 %copy-start.3 = (s32[64,1]{0,1:T(1,128)S(1)}, s32[64,1]{0,1:T(1,128)}, u32[]{:S(2)}) copy-start(s32[64,1]{0,1:T(1,128)} %param.10) | copy-start | bytes 772
  19.2 20.7 %copy-start.2 = (bf16[64,64,128]{2,1,0:T(8,128)(2,1)S(1)}, bf16[64,64,128]{2,1,0:T(8,128)(2,1)}, u32[]{:S(2)}) copy-start(bf16[64,64,128]{2,1,0:T(8,128)(2,1)} %param.9) | copy-start | bytes 3145732
  29.1 25.6 %all-to-all-start.1 = ((bf16[8,64,1024]{2,1,0:T(8,128)(2,1)}), bf16[8,64,1024]{2,1,0:T(8,128)(2,1)S(1)}, u32[]{:S(2)}, u32[]{:S(2)}) async-start(bf16[8,64,1024]{2,1,0:T(8,128)(2,1)} %bitcast.4), calls=%async_computation.1 | async-start | bytes 2097152 | tf_op jit(solution)/shard_map/all_to_all | solution.py:23
  54.7 38.0 %all-to-all-start.7 = ((bf16[16,8,2048]{2,1,0:T(8,128)(2,1)}), bf16[16,8,2048]{2,1,0:T(8,128)(2,1)S(1)}, u32[]{:S(2)}, u32[]{:S(2)}) async-start(bf16[16,8,2048]{2,1,0:T(8,128)(2,1)} %fusion.2), calls=%async_computation.7 | async-start | bytes 1048576 | tf_op jit(solution)/shard_map/all_to_all | solution.py:23
  92.7 56.7 %copy-start.1 = (bf16[16,8,2048]{2,1,0:T(8,128)(2,1)}, bf16[16,8,2048]{2,1,0:T(8,128)(2,1)S(1)}, u32[]{:S(2)}) copy-start(bf16[16,8,2048]{2,1,0:T(8,128)(2,1)S(1)} %all-to-all-done.7) | copy-start | bytes 1572868
  149.4 28.6 %all-to-all-start.4 = ((bf16[4,4,64,1024]{3,2,1,0:T(8,128)(2,1)}), bf16[4,4,64,1024]{3,2,1,0:T(8,128)(2,1)S(1)}, u32[]{:S(2)}, u32[]{:S(2)}) async-start(bf16[4,4,64,1024]{3,2,1,0:T(8,128)(2,1)} %broadcast_in_dim.32), calls=%async_computation.4 | async-start | bytes 4194304 | tf_op jit(solution)/shard_map/all_to_all | solution.py:23
  177.9 11.2 %all-to-all-start.8 = ((bf16[4,32,2048]{2,1,0:T(8,128)(2,1)}), bf16[4,32,2048]{2,1,0:T(8,128)(2,1)}, u32[]{:S(2)}, u32[]{:S(2)}) async-start(bf16[4,32,2048]{2,1,0:T(8,128)(2,1)} %copy.30), calls=%async_computation.8 | async-start | bytes 1048576 | tf_op jit(solution)/shard_map/all_to_all | solution.py:23
  189.1 21.9 %all-to-all-start.5 = ((f32[8,256,128]{2,1,0:T(8,128)}), f32[8,256,128]{2,1,0:T(8,128)S(1)}, u32[]{:S(2)}, u32[]{:S(2)}) async-start(f32[8,256,128]{2,1,0:T(8,128)} %bitcast.11), calls=%async_computation.5 | async-start | bytes 2097152 | tf_op jit(solution)/shard_map/all_to_all | solution.py:23
  211.7 10.8 %all-to-all-start.9 = ((f32[8,64,128]{2,1,0:T(8,128)}), f32[8,64,128]{2,1,0:T(8,128)S(1)}, u32[]{:S(2)}, u32[]{:S(2)}) async-start(f32[8,64,128]{2,1,0:T(8,128)} %broadcast_in_dim.33), calls=%async_computation.9 | async-start | bytes 524288 | tf_op jit(solution)/shard_map/all_to_all | solution.py:23
  222.5 9.3 %all-to-all-start.6 = ((f32[4,64,128]{2,1,0:T(8,128)}), f32[4,64,128]{2,1,0:T(8,128)S(1)}, u32[]{:S(2)}, u32[]{:S(2)}) async-start(f32[4,64,128]{2,1,0:T(8,128)} %bitcast.12), calls=%async_computation.6 | async-start | bytes 262144 | tf_op jit(solution)/shard_map/all_to_all | solution.py:23

commit v2 on v1

--- a/solution.py
+++ b/solution.py
@@ -5,6 +5,7 @@
 from jax import lax
 from jax.sharding import Mesh
 from jax.sharding import PartitionSpec as P
+
 
 VW = 1024
 R = 16
@@ -25,6 +26,22 @@
 
 def from_everyone(value, axes):
     return swap(jnp.broadcast_to(value, (lax.axis_size(axes), *value.shape)), axes)
+
+
+def shifted(value, axes, shift):
+    size = lax.axis_size(axes)
+    return lax.ppermute(value, axes, [(k, (k + shift) % size) for k in range(size)])
+
+
+def placed_at(parts, places):
+    out = jnp.zeros((len(parts), *parts[0].shape), parts[0].dtype)
+    for part, place in zip(parts, places, strict=True):
+        out = lax.dynamic_update_slice_in_dim(out, part[None], place, 0)
+    return out
+
+
+def part_of(parts, place):
+    return lax.dynamic_index_in_dim(parts, place, 0, keepdims=False)
 
 
 def sign_table(coords, columns, seed_word):
@@ -50,7 +67,9 @@
     coords_here = R * width
 
     train_grads = local_grads(train_in, train_out_grad)
-    by_y = from_everyone(train_grads, "y")
+    x, y, c, zh, _ = (lax.axis_index(a) for a in ("x", "y", "c", "zh", "zl"))
+    by_y = [train_grads] + [shifted(train_grads, "y", -k) for k in range(1, ny)]
+    by_y = jnp.stack(by_y).reshape(ny * examples, coords_here)
 
     query_grads = local_grads(query_in, query_out_grad)
     owners = query_owner[:, 0]
@@ -71,37 +90,54 @@
     arrived = arrived.reshape(nz, ny, capacity, coords_here).swapaxes(0, 1)
 
     seed_word = sketch_seed[0]
-    block_cols = K // ny
-    columns = lax.axis_index("y") * block_cols + lax.iota(jnp.int32, block_cols)
+    half_cols = K // ny // nc
     first = lax.axis_index(MP) * width
     coords = (
         lax.broadcasted_iota(jnp.int32, (R, width), 0) * VW
         + lax.broadcasted_iota(jnp.int32, (R, width), 1)
         + first
     ).reshape(-1)
-    signs = lax.optimization_barrier(sign_table(coords, columns, seed_word))
-    partial = jnp.dot(
-        by_y.reshape(ny * examples, coords_here), signs, preferred_element_type=jnp.float32
+    halves = []
+    for half in (1 - c, c):
+        columns = (y * nc + half) * half_cols + lax.iota(jnp.int32, half_cols)
+        signs = sign_table(coords, columns, seed_word)
+        signs = lax.optimization_barrier(signs)
+        halves.append(jnp.dot(by_y, signs, preferred_element_type=jnp.float32))
+    traded = shifted(halves[0].astype(jnp.bfloat16), "c", 1)
+    partial = lax.optimization_barrier(halves[1]) + traded.astype(jnp.float32)
+    partial = partial.reshape(ny, examples, half_cols)
+    turn = x - y + ny
+    features = part_of(partial, lax.rem(turn, ny))
+    sent = [
+        shifted(part_of(partial, lax.rem(turn + k, ny)).astype(jnp.bfloat16), "x", k)
+        for k in range(1, nx)
+    ]
+    for part in sent:
+        features = features + part.astype(jnp.float32)
+    feature_scale = 1.0 / math.sqrt(L * R * VW)
+    features = (features * feature_scale).astype(jnp.bfloat16)
+
+    near = from_everyone(features, "zl").reshape(nzl * examples, -1)
+    above, below = shifted(features, Z, -nzl), shifted(features, Z, nzl)
+    cols = jnp.stack([near] + [shifted(near, "x", -k) for k in range(1, nx)])
+    cut = examples // 2
+    opposite = [shifted(above[:cut], Z, -nzl), shifted(below[cut:], Z, nzl)]
+    opposite = jnp.concatenate(opposite, axis=0)
+    rows = placed_at(
+        [features, above, opposite, below], [lax.rem(zh + k, nzh) ^ (c * 2) for k in range(nzh)]
     )
-    partial = partial.astype(jnp.bfloat16).reshape(ny, examples, nc, block_cols // nc)
-    partial = partial.transpose(0, 2, 1, 3).reshape(ny * nc, examples, block_cols // nc)
-    feature_scale = 1.0 / math.sqrt(L * R * VW)
-    features = (swap(partial, MP).astype(jnp.float32).sum(axis=0) * feature_scale).astype(
-        jnp.bfloat16
+    rows = rows.reshape(nc, (nzh // nc) * examples, -1)
+    kept, given = (
+        jnp.einsum("tmk,nk->tmn", cols, rows[h], preferred_element_type=jnp.float32)
+        for h in range(nc)
     )
-
-    near = from_everyone(features, "zl")
-    rows = from_everyone(features, "zh")
-    cols = from_everyone(near, "x")
-    depth = features.shape[1]
-    gram = jnp.einsum(
-        "ymk,ank->yamn",
-        cols.reshape(nx, nzl * examples, depth),
-        rows.reshape(nc, (nzh // nc) * examples, depth),
-        preferred_element_type=jnp.float32,
-    )
-    gram = swap(gram.reshape(ny * nc, nzl * examples, -1), ("y", "c")).sum(axis=0)
-    gram = swap(gram.reshape(nzl, examples, -1), "zl") * (1.0 / math.sqrt(K))
+    traded = shifted(given.astype(jnp.bfloat16), "c", 1)
+    gram = lax.optimization_barrier(kept) + traded.astype(jnp.float32)
+    gram = jnp.stack([part_of(gram, lax.rem(k - x + nx, nx)) for k in range(ny)])
+    gram = gram.astype(jnp.bfloat16).reshape(ny * nzl, examples, -1)
+    gram = swap(gram, ("y", "zl"))
+    gram = gram.reshape(ny, nzl, examples, -1).astype(jnp.float32).sum(axis=0)
+    gram = gram * (1.0 / math.sqrt(K))
     gram = gram.reshape(nzl, examples, nzh // nc, examples).transpose(2, 0, 3, 1)
     gram = gram.reshape(-1, examples)
 
@@ -113,7 +149,8 @@
         preferred_element_type=jnp.float32,
     )
     score_scale = 1.0 / (L * math.sqrt(R * VW))
-    scores = from_everyone(scores.reshape(-1, 2 * examples), MP).sum(axis=0) * score_scale
+    scores = from_everyone(scores.reshape(-1, 2 * examples), MP)
+    scores = scores.sum(axis=0) * score_scale
     return gram, scores.reshape(1, ny * nz, capacity, examples)
 
 

time: 234 us -> 176 us (0.75)
  blocking collectives: 55 us -> 0 us
  starting transfers between devices: 53.9 us -> 102 us
  waiting for transfers between devices: 85.7 us -> 38.6 us
  local copies, waits for them, and re-layouts: 15.3 us -> 8.19 us
  other arithmetic: 6.97 us -> 10 us
    all_to_all x8 -> x5, waiting for transfers between devices: 85.7 us -> 9.28 us  [swap(): return lax.all_to_all(parts, axes, split_axis=0, concat_axis=0, tiled=True)]
    all_to_all x2 -> x0, blocking collectives: 55 us -> none  [swap(): return lax.all_to_all(parts, axes, split_axis=0, concat_axis=0, tiled=True)]
    ppermute x0 -> x15, starting transfers between devices: none -> 54.3 us  [shifted(): lax.ppermute(value, axes, [(k, (k + shift) % size) for k in range(size)])]
    ppermute x0 -> x15, waiting for transfers between devices: none -> 29.3 us  [shifted(): lax.ppermute(value, axes, [(k, (k + shift) % size) for k in range(size)])]
    all_to_all x8 -> x5, starting transfers between devices: 53.9 us -> 47.9 us  [swap(): return lax.all_to_all(parts, axes, split_axis=0, concat_axis=0, tiled=True)]
    reshape x4 -> x1, local copies, waits for them, and re-layouts: 3.34 us -> 0.07 us  [shards(): scores = from_everyone(scores.reshape(-1, 2 * examples), MP)]
    transpose x1 -> x0, local copies, waits for them, and re-layouts: 2.53 us -> none  [shards(): jnp.einsum('ymk,ank->yamn', cols.reshape(nx, nzl * examples, depth), rows...]
    dot_general x2 -> x4, matrix products: 9.67 us -> 9.73 us  [the longest x2 5.52 us: shards(): halves.append(jnp.dot(by_y, signs, preferred_element_type=jnp.float32))]
  transfers between devices with their start and end apart: 8 -> 20, of which waited for: 8 -> 9; matrix products, arithmetic and copies ran while one was open for 8% -> 15% of each run, Pallas kernels for 0% -> 0%
where the time goes in v2:
time: 176 us; the launch traced here: 175 us
  starting transfers between devices  102 us (58%)
  waiting for transfers between devices  38.6 us (22%)
  matrix products  14.1 us (8%)
  other arithmetic  10 us (6%)
  local copies, waits for them, and re-layouts  8.19 us (5%)
  between operations  1.78 us (1%)
    ppermute x15, starting transfers between devices, shifted(): lax.ppermute(value, axes, [(k, (k + shift) % size) for k in range(size)])  54.3 us
    all_to_all x5, starting transfers between devices, swap(): return lax.all_to_all(parts, axes, split_axis=0, concat_axis=0, tiled=True)  47.9 us
    ppermute x15, waiting for transfers between devices, shifted(): lax.ppermute(value, axes, [(k, (k + shift) % size) for k in range(size)])  29.3 us
    all_to_all x5, waiting for transfers between devices, swap(): return lax.all_to_all(parts, axes, split_axis=0, concat_axis=0, tiled=True)  9.28 us
    dot_general x2, matrix products, shards(): halves.append(jnp.dot(by_y, signs, preferred_element_type=jnp.float32))  5.52 us
    convert_element_type x1, other arithmetic, sign_table(): return jnp.where(mixed < 0, -1.0, 1.0).astype(jnp.bfloat16)  5.09 us
    dot_general x2, matrix products, shards(): jnp.einsum('tmk,nk->tmn', cols, rows[h], preferred_element_type=jnp.float32)  4.2 us
  transfers between devices with their start and end apart: 20, of which 9 were waited for; matrix products, arithmetic and copies ran while one was open for 15% of the time, Pallas kernels for 0%

profile of v2, /device:TPU:1, one launch (start us, length us, event | category | flops | bytes accessed | tf_op | source)
XLA Modules:
  0.0 174.8 jit_solution(3527081590067477843)
XLA Ops:
  3.2 5.5 %collective-permute-start = (bf16[64,16,128]{2,1,0:T(8,128)(2,1)S(1)}, bf16[64,16,128]{2,1,0:T(8,128)(2,1)S(1)}, u32[]{:S(2)}, u32[]{:S(2)}) collective-permute-start(bf16[64,16,128]{2,1,0:T(8,128)(2,1)S(1)} %convolution_convert_fusion.4), channel_id=1, source_target_pairs={{0,384},{128,0},{256,128},{384,256},{1,385},{129,1},{257,129},{385... | collective-permute-start | bytes 786440 | tf_op jit(solution)/shard_map/ppermute | solution.py:33
  8.7 2.3 %collective-permute-start.1 = (bf16[64,16,128]{2,1,0:T(8,128)(2,1)S(1)}, bf16[64,16,128]{2,1,0:T(8,128)(2,1)S(1)}, u32[]{:S(2)}, u32[]{:S(2)}) collective-permute-start(bf16[64,16,128]{2,1,0:T(8,128)(2,1)S(1)} %convolution_convert_fusion.4), channel_id=1, source_target_pairs={{0,256},{128,384},{256,0},{384,128},{1,257},{129,385},{257,1},{385... | collective-permute-start | bytes 786440 | tf_op jit(solution)/shard_map/ppermute | solution.py:33
  10.9 2.6 %collective-permute-start.2 = (bf16[64,16,128]{2,1,0:T(8,128)(2,1)S(1)}, bf16[64,16,128]{2,1,0:T(8,128)(2,1)}, u32[]{:S(2)}, u32[]{:S(2)}) collective-permute-start(bf16[64,16,128]{2,1,0:T(8,128)(2,1)S(1)} %convolution_convert_fusion.4), channel_id=1, source_target_pairs={{0,128},{128,256},{256,384},{384,0},{1,129},{129,257},{257,385},{3... | collective-permute-start | bytes 786440 | tf_op jit(solution)/shard_map/ppermute | solution.py:33
  15.1 1.7 convolution_convert_fusion.2
  17.9 14.9 %all-to-all-start.2 = ((bf16[16,8,2048]{2,1,0:T(8,128)(2,1)}), bf16[16,8,2048]{2,1,0:T(8,128)(2,1)S(1)}, u32[]{:S(2)}, u32[]{:S(2)}) async-start(bf16[16,8,2048]{2,1,0:T(8,128)(2,1)} %fusion.4), calls=%async_computation.2 | async-start | bytes 1048576 | tf_op jit(solution)/shard_map/all_to_all | solution.py:24
  33.6 5.1 %select_convert_fusion = (bf16[2048,1024]{1,0:T(8,128)(2,1)S(1)}, bf16[2048,1024]{1,0:T(8,128)(2,1)}) fusion(s32[1024]{0:T(1024)S(1)} %get-tuple-element.15, s32[2048]{0:T(1024)S(1)} %multiply_bitcast_fusion, s32[1024]{0:T(1024)S(1)} %get-tuple-element.16), kind=kLoop, calls=%fused_computation.6 | loop fusion | flops 29360128 | bytes 8404992 | tf_op jit(solution)/shard_map/convert_element_type | solution.py:53
  39.8 2.1 %convolution_convert_fusion.1 = bf16[256,1024]{1,0:T(8,128)(2,1)} fusion(bf16[2048,1024]{1,0:T(8,128)(2,1)S(1)} %get-tuple-element.13, bf16[32,8,16,128]{3,2,1,0:T(8,128)(2,1)S(1)} %bitcast.90), kind=kOutput, calls=%fused_computation.11 | convolution fusion | flops 1074003968 | bytes 5767168 | tf_op jit(solution)/shard_map/dot_general | solution.py:105
  41.9 3.7 %collective-permute-start.3 = (bf16[256,1024]{1,0:T(8,128)(2,1)}, bf16[256,1024]{1,0:T(8,128)(2,1)S(1)}, u32[]{:S(2)}, u32[]{:S(2)}) collective-permute-start(bf16[256,1024]{1,0:T(8,128)(2,1)} %convolution_convert_fusion.1), channel_id=1, source_target_pairs={{0,1},{1,0},{2,3},{3,2},{4,5},{5,4},{6,7},{7,6},{8,9},{9,8},{10,11... | collective-permute-start | bytes 1572872 | tf_op jit(solution)/shard_map/ppermute | solution.py:33
  45.6 3.4 %fusion.6 = f32[256,1024]{1,0:T(8,128)S(1)} fusion(bf16[2048,1024]{1,0:T(8,128)(2,1)} %get-tuple-element.14, bf16[32,8,16,128]{3,2,1,0:T(8,128)(2,1)S(1)} %bitcast.91), kind=kOutput, calls=%fused_computation.16 | convolution fusion | flops 1073741824 | bytes 6291456 | tf_op jit(solution)/shard_map/dot_general | solution.py:105
  49.3 3.1 %collective-permute-start.4 = (bf16[64,1024]{1,0:T(8,128)(2,1)S(1)}, bf16[64,1024]{1,0:T(8,128)(2,1)}, u32[]{:S(2)}, u32[]{:S(2)}) collective-permute-start(bf16[64,1024]{1,0:T(8,128)(2,1)S(1)} %get-tuple-element.4), channel_id=1, source_target_pairs={{0,2},{2,4},{4,6},{6,0},{1,3},{3,5},{5,7},{7,1},{8,10},{10,12},{12... | collective-permute-start | bytes 393224 | tf_op jit(solution)/shard_map/ppermute | solution.py:33
  52.5 4.4 %collective-permute-start.5 = (bf16[64,1024]{1,0:T(8,128)(2,1)S(1)}, bf16[64,1024]{1,0:T(8,128)(2,1)S(1)}, u32[]{:S(2)}, u32[]{:S(2)}) collective-permute-start(bf16[64,1024]{1,0:T(8,128)(2,1)S(1)} %get-tuple-element.6), channel_id=1, source_target_pairs={{0,4},{2,6},{4,0},{6,2},{1,5},{3,7},{5,1},{7,3},{8,12},{10,14},{12... | collective-permute-start | bytes 393224 | tf_op jit(solution)/shard_map/ppermute | solution.py:33
  56.8 3.1 %collective-permute-start.6 = (bf16[64,1024]{1,0:T(8,128)(2,1)S(1)}, bf16[64,1024]{1,0:T(8,128)(2,1)}, u32[]{:S(2)}, u32[]{:S(2)}) collective-permute-start(bf16[64,1024]{1,0:T(8,128)(2,1)S(1)} %get-tuple-element.5), channel_id=1, source_target_pairs={{0,6},{2,0},{4,2},{6,4},{1,7},{3,1},{5,3},{7,5},{8,14},{10,8},{12,... | collective-permute-start | bytes 393224 | tf_op jit(solution)/shard_map/ppermute | solution.py:33
  59.9 1.4 collective-permute-done.5
  65.3 4.7 %all-to-all-start = ((bf16[4,64,1024]{2,1,0:T(8,128)(2,1)}), bf16[4,64,1024]{2,1,0:T(8,128)(2,1)S(1)}, u32[]{:S(2)}, u32[]{:S(2)}) async-start(bf16[4,64,1024]{2,1,0:T(8,128)(2,1)} %broadcast_in_dim.38), calls=%async_computation | async-start | bytes 1048576 | tf_op jit(solution)/shard_map/all_to_all | solution.py:24
  70.1 6.2 %collective-permute-start.10 = (bf16[64,1024]{1,0:T(8,128)(2,1)S(1)}, bf16[64,1024]{1,0:T(8,128)(2,1)S(1)}, u32[]{:S(2)}, u32[]{:S(2)}) collective-permute-start(bf16[64,1024]{1,0:T(8,128)(2,1)S(1)} %get-tuple-element.3), channel_id=1, source_target_pairs={{0,96},{8,104},{16,112},{24,120},{32,0},{40,8},{48,16},{56,24},{64... | collective-permute-start | bytes 393224 | tf_op jit(solution)/shard_map/ppermute | solution.py:33
  76.3 2.9 %collective-permute-start.12 = (bf16[64,1024]{1,0:T(8,128)(2,1)S(1)}, bf16[64,1024]{1,0:T(8,128)(2,1)S(1)}, u32[]{:S(2)}, u32[]{:S(2)}) collective-permute-start(bf16[64,1024]{1,0:T(8,128)(2,1)S(1)} %get-tuple-element.3), channel_id=1, source_target_pairs={{0,32},{8,40},{16,48},{24,56},{32,64},{40,72},{48,80},{56,88},{64,... | collective-permute-start | bytes 393224 | tf_op jit(solution)/shard_map/ppermute | solution.py:33
  79.9 6.1 %collective-permute-start.11 = (bf16[32,1024]{1,0:T(8,128)(2,1)S(1)}, bf16[32,1024]{1,0:T(8,128)(2,1)S(1)}, u32[]{:S(2)}, u32[]{:S(2)}) collective-permute-start(bf16[32,1024]{1,0:T(8,128)(2,1)S(1)} %slice.18), channel_id=1, source_target_pairs={{0,96},{8,104},{16,112},{24,120},{32,0},{40,8},{48,16},{56,24},{64... | collective-permute-start | bytes 196616 | tf_op jit(solution)/shard_map/ppermute | solution.py:33
  86.2 3.0 %collective-permute-start.13 = (bf16[32,1024]{1,0:T(8,128)(2,1)S(1)}, bf16[32,1024]{1,0:T(8,128)(2,1)S(1)}, u32[]{:S(2)}, u32[]{:S(2)}) collective-permute-start(bf16[32,1024]{1,0:T(8,128)(2,1)S(1)} %slice.19), channel_id=1, source_target_pairs={{0,32},{8,40},{16,48},{24,56},{32,64},{40,72},{48,80},{56,88},{64,... | collective-permute-start | bytes 196616 | tf_op jit(solution)/shard_map/ppermute | solution.py:33
  89.2 1.9 %collective-permute-done.11 = bf16[32,1024]{1,0:T(8,128)(2,1)S(1)} collective-permute-done((bf16[32,1024]{1,0:T(8,128)(2,1)S(1)}, bf16[32,1024]{1,0:T(8,128)(2,1)S(1)}, u32[]{:S(2)}, u32[]{:S(2)}) %collective-permute-start.11) | collective-permute-done | bytes 65568 | tf_op jit(solution)/shard_map/ppermute | solution.py:33
  91.1 7.4 %collective-permute-done.13 = bf16[32,1024]{1,0:T(8,128)(2,1)S(1)} collective-permute-done((bf16[32,1024]{1,0:T(8,128)(2,1)S(1)}, bf16[32,1024]{1,0:T(8,128)(2,1)S(1)}, u32[]{:S(2)}, u32[]{:S(2)}) %collective-permute-start.13) | collective-permute-done | bytes 65568 | tf_op jit(solution)/shard_map/ppermute | solution.py:33
  100.4 3.5 %all-to-all-start.3 = ((bf16[4,32,2048]{2,1,0:T(8,128)(2,1)}), bf16[4,32,2048]{2,1,0:T(8,128)(2,1)S(1)}, u32[]{:S(2)}, u32[]{:S(2)}) async-start(bf16[4,32,2048]{2,1,0:T(8,128)(2,1)} %copy.22), calls=%async_computation.3 | async-start | bytes 1048576 | tf_op jit(solution)/shard_map/all_to_all | solution.py:24
  103.9 4.3 %collective-permute-start.7 = (bf16[256,1024]{1,0:T(8,128)(2,1)S(1)}, bf16[256,1024]{1,0:T(8,128)(2,1)}, u32[]{:S(2)}, u32[]{:S(2)}) collective-permute-start(bf16[256,1024]{1,0:T(8,128)(2,1)S(1)} %bitcast.97), channel_id=1, source_target_pairs={{0,6},{2,0},{4,2},{6,4},{1,7},{3,1},{5,3},{7,5},{8,14},{10,8},{12,... | collective-permute-start | bytes 1572872 | tf_op jit(solution)/shard_map/ppermute | solution.py:33
  108.1 2.4 %collective-permute-start.8 = (bf16[256,1024]{1,0:T(8,128)(2,1)S(1)}, bf16[256,1024]{1,0:T(8,128)(2,1)}, u32[]{:S(2)}, u32[]{:S(2)}) collective-permute-start(bf16[256,1024]{1,0:T(8,128)(2,1)S(1)} %bitcast.98), channel_id=1, source_target_pairs={{0,4},{2,6},{4,0},{6,2},{1,5},{3,7},{5,1},{7,3},{8,12},{10,14},{12... | collective-permute-start | bytes 1572872 | tf_op jit(solution)/shard_map/ppermute | solution.py:33
  110.5 2.3 %collective-permute-start.9 = (bf16[256,1024]{1,0:T(8,128)(2,1)S(1)}, bf16[256,1024]{1,0:T(8,128)(2,1)}, u32[]{:S(2)}, u32[]{:S(2)}) collective-permute-start(bf16[256,1024]{1,0:T(8,128)(2,1)S(1)} %bitcast.99), channel_id=1, source_target_pairs={{0,2},{2,4},{4,6},{6,0},{1,3},{3,5},{5,7},{7,1},{8,10},{10,12},{12... | collective-permute-start | bytes 1572872 | tf_op jit(solution)/shard_map/ppermute | solution.py:33
  114.7 6.3 %all-to-all-start.4 = ((f32[8,64,128]{2,1,0:T(8,128)}), f32[8,64,128]{2,1,0:T(8,128)S(1)}, u32[]{:S(2)}, u32[]{:S(2)}) async-start(f32[8,64,128]{2,1,0:T(8,128)} %broadcast_in_dim.44), calls=%async_computation.4 | async-start | bytes 524288 | tf_op jit(solution)/shard_map/all_to_all | solution.py:24
  121.0 2.3 %collective-permute-done.8 = bf16[256,1024]{1,0:T(8,128)(2,1)} collective-permute-done((bf16[256,1024]{1,0:T(8,128)(2,1)S(1)}, bf16[256,1024]{1,0:T(8,128)(2,1)}, u32[]{:S(2)}, u32[]{:S(2)}) %collective-permute-start.8) | collective-permute-done | bytes 524320 | tf_op jit(solution)/shard_map/ppermute | solution.py:33
  123.3 14.1 %collective-permute-done.9 = bf16[256,1024]{1,0:T(8,128)(2,1)} collective-permute-done((bf16[256,1024]{1,0:T(8,128)(2,1)S(1)}, bf16[256,1024]{1,0:T(8,128)(2,1)}, u32[]{:S(2)}, u32[]{:S(2)}) %collective-permute-start.9) | collective-permute-done | bytes 524320 | tf_op jit(solution)/shard_map/ppermute | solution.py:33
  137.4 2.1 %convolution_convert_fusion.3 = bf16[4,256,128]{2,1,0:T(8,128)(2,1)S(1)} fusion(bf16[128,1024,1]{1,0,2:T(8,128)(2,1)} %bitcast.104, bf16[1,256,1024]{2,1,0:T(8,128)(2,1)} %bitcast.16, bf16[1,256,1024]{2,1,0:T(8,128)(2,1)} %bitcast.15, bf16[1,256,1024]{2,1,0:T(8,128)(2,1)} %bitcast.14, bf16[1,256,1024]{2,1,0:T(8,128)(2,1)S(1)} %bitcast.100), kind=kOutput, calls=%fused_computation.13 | convolution fusion | flops 271712256 | bytes 2621440 | tf_op jit(solution)/shard_map/tmk,nk->tmn/dot_general | solution.py:131
  139.6 2.5 %collective-permute-start.14 = (bf16[4,256,128]{2,1,0:T(8,128)(2,1)S(1)}, bf16[4,256,128]{2,1,0:T(8,128)(2,1)S(1)}, u32[]{:S(2)}, u32[]{:S(2)}) collective-permute-start(bf16[4,256,128]{2,1,0:T(8,128)(2,1)S(1)} %convolution_convert_fusion.3), channel_id=1, source_target_pairs={{0,1},{1,0},{2,3},{3,2},{4,5},{5,4},{6,7},{7,6},{8,9},{9,8},{10,11... | collective-permute-start | bytes 786440 | tf_op jit(solution)/shard_map/ppermute | solution.py:33
  142.1 2.1 %fusion.10 = f32[4,256,128]{2,1,0:T(8,128)S(1)} fusion(bf16[128,1024,1]{1,0,2:T(8,128)(2,1)S(1)} %bitcast.103, bf16[1,256,1024]{2,1,0:T(8,128)(2,1)} %bitcast.16, bf16[1,256,1024]{2,1,0:T(8,128)(2,1)} %bitcast.15, bf16[1,256,1024]{2,1,0:T(8,128)(2,1)} %bitcast.14, bf16[1,256,1024]{2,1,0:T(8,128)(2,1)S(1)} %bitcast.101), kind=kOutput, calls=%fused_computation.24 | convolution fusion | flops 271581184 | bytes 2883584 | tf_op jit(solution)/shard_map/tmk,nk->tmn/dot_general | solution.py:131
  145.0 18.5 %all-to-all-start.1 = ((bf16[16,64,128]{2,1,0:T(8,128)(2,1)}), bf16[16,64,128]{2,1,0:T(8,128)(2,1)S(1)}, u32[]{:S(2)}, u32[]{:S(2)}) async-start(bf16[16,64,128]{2,1,0:T(8,128)(2,1)} %bitcast.25), calls=%async_computation.1 | async-start | bytes 524288 | tf_op jit(solution)/shard_map/all_to_all | solution.py:24
  164.3 9.3 %all-to-all-done.1 = bf16[16,64,128]{2,1,0:T(8,128)(2,1)S(1)} async-done(((bf16[16,64,128]{2,1,0:T(8,128)(2,1)}), bf16[16,64,128]{2,1,0:T(8,128)(2,1)S(1)}, u32[]{:S(2)}, u32[]{:S(2)}) %all-to-all-start.1) | async-done | bytes 262176 | tf_op jit(solution)/shard_map/all_to_all | solution.py:24
  (54 shorter events, 17.9 us)
Async XLA Ops:
  0.6 1.2 copy-start
  3.2 35.5 %collective-permute-start = (bf16[64,16,128]{2,1,0:T(8,128)(2,1)S(1)}, bf16[64,16,128]{2,1,0:T(8,128)(2,1)S(1)}, u32[]{:S(2)}, u32[]{:S(2)}) collective-permute-start(bf16[64,16,128]{2,1,0:T(8,128)(2,1)S(1)} %convolution_convert_fusion.4), channel_id=1, source_target_pairs={{0,384},{128,0},{256,128},{384,256},{1,385},{129,1},{257,129},{385... | collective-permute-start | bytes 786440 | tf_op jit(solution)/shard_map/ppermute | solution.py:33
  8.7 30.1 %collective-permute-start.1 = (bf16[64,16,128]{2,1,0:T(8,128)(2,1)S(1)}, bf16[64,16,128]{2,1,0:T(8,128)(2,1)S(1)}, u32[]{:S(2)}, u32[]{:S(2)}) collective-permute-start(bf16[64,16,128]{2,1,0:T(8,128)(2,1)S(1)} %convolution_convert_fusion.4), channel_id=1, source_target_pairs={{0,256},{128,384},{256,0},{384,128},{1,257},{129,385},{257,1},{385... | collective-permute-start | bytes 786440 | tf_op jit(solution)/shard_map/ppermute | solution.py:33
  10.9 27.8 %collective-permute-start.2 = (bf16[64,16,128]{2,1,0:T(8,128)(2,1)S(1)}, bf16[64,16,128]{2,1,0:T(8,128)(2,1)}, u32[]{:S(2)}, u32[]{:S(2)}) collective-permute-start(bf16[64,16,128]{2,1,0:T(8,128)(2,1)S(1)} %convolution_convert_fusion.4), channel_id=1, source_target_pairs={{0,128},{128,256},{256,384},{384,0},{1,129},{129,257},{257,385},{3... | collective-permute-start | bytes 786440 | tf_op jit(solution)/shard_map/ppermute | solution.py:33
  17.9 46.5 %all-to-all-start.2 = ((bf16[16,8,2048]{2,1,0:T(8,128)(2,1)}), bf16[16,8,2048]{2,1,0:T(8,128)(2,1)S(1)}, u32[]{:S(2)}, u32[]{:S(2)}) async-start(bf16[16,8,2048]{2,1,0:T(8,128)(2,1)} %fusion.4), calls=%async_computation.2 | async-start | bytes 1048576 | tf_op jit(solution)/shard_map/all_to_all | solution.py:24
  41.9 7.2 %collective-permute-start.3 = (bf16[256,1024]{1,0:T(8,128)(2,1)}, bf16[256,1024]{1,0:T(8,128)(2,1)S(1)}, u32[]{:S(2)}, u32[]{:S(2)}) collective-permute-start(bf16[256,1024]{1,0:T(8,128)(2,1)} %convolution_convert_fusion.1), channel_id=1, source_target_pairs={{0,1},{1,0},{2,3},{3,2},{4,5},{5,4},{6,7},{7,6},{8,9},{9,8},{10,11... | collective-permute-start | bytes 1572872 | tf_op jit(solution)/shard_map/ppermute | solution.py:33
  49.3 10.6 %collective-permute-start.4 = (bf16[64,1024]{1,0:T(8,128)(2,1)S(1)}, bf16[64,1024]{1,0:T(8,128)(2,1)}, u32[]{:S(2)}, u32[]{:S(2)}) collective-permute-start(bf16[64,1024]{1,0:T(8,128)(2,1)S(1)} %get-tuple-element.4), channel_id=1, source_target_pairs={{0,2},{2,4},{4,6},{6,0},{1,3},{3,5},{5,7},{7,1},{8,10},{10,12},{12... | collective-permute-start | bytes 393224 | tf_op jit(solution)/shard_map/ppermute | solution.py:33
  52.5 8.9 %collective-permute-start.5 = (bf16[64,1024]{1,0:T(8,128)(2,1)S(1)}, bf16[64,1024]{1,0:T(8,128)(2,1)S(1)}, u32[]{:S(2)}, u32[]{:S(2)}) collective-permute-start(bf16[64,1024]{1,0:T(8,128)(2,1)S(1)} %get-tuple-element.6), channel_id=1, source_target_pairs={{0,4},{2,6},{4,0},{6,2},{1,5},{3,7},{5,1},{7,3},{8,12},{10,14},{12... | collective-permute-start | bytes 393224 | tf_op jit(solution)/shard_map/ppermute | solution.py:33
  56.8 6.5 %collective-permute-start.6 = (bf16[64,1024]{1,0:T(8,128)(2,1)S(1)}, bf16[64,1024]{1,0:T(8,128)(2,1)}, u32[]{:S(2)}, u32[]{:S(2)}) collective-permute-start(bf16[64,1024]{1,0:T(8,128)(2,1)S(1)} %get-tuple-element.5), channel_id=1, source_target_pairs={{0,6},{2,0},{4,2},{6,4},{1,7},{3,1},{5,3},{7,5},{8,14},{10,8},{12,... | collective-permute-start | bytes 393224 | tf_op jit(solution)/shard_map/ppermute | solution.py:33
  61.4 0.7 copy-start.1
  65.3 35.0 %all-to-all-start = ((bf16[4,64,1024]{2,1,0:T(8,128)(2,1)}), bf16[4,64,1024]{2,1,0:T(8,128)(2,1)S(1)}, u32[]{:S(2)}, u32[]{:S(2)}) async-start(bf16[4,64,1024]{2,1,0:T(8,128)(2,1)} %broadcast_in_dim.38), calls=%async_computation | async-start | bytes 1048576 | tf_op jit(solution)/shard_map/all_to_all | solution.py:24
  70.1 9.8 %collective-permute-start.10 = (bf16[64,1024]{1,0:T(8,128)(2,1)S(1)}, bf16[64,1024]{1,0:T(8,128)(2,1)S(1)}, u32[]{:S(2)}, u32[]{:S(2)}) collective-permute-start(bf16[64,1024]{1,0:T(8,128)(2,1)S(1)} %get-tuple-element.3), channel_id=1, source_target_pairs={{0,96},{8,104},{16,112},{24,120},{32,0},{40,8},{48,16},{56,24},{64... | collective-permute-start | bytes 393224 | tf_op jit(solution)/shard_map/ppermute | solution.py:33
  76.3 9.9 %collective-permute-start.12 = (bf16[64,1024]{1,0:T(8,128)(2,1)S(1)}, bf16[64,1024]{1,0:T(8,128)(2,1)S(1)}, u32[]{:S(2)}, u32[]{:S(2)}) collective-permute-start(bf16[64,1024]{1,0:T(8,128)(2,1)S(1)} %get-tuple-element.3), channel_id=1, source_target_pairs={{0,32},{8,40},{16,48},{24,56},{32,64},{40,72},{48,80},{56,88},{64,... | collective-permute-start | bytes 393224 | tf_op jit(solution)/shard_map/ppermute | solution.py:33
  79.9 11.2 %collective-permute-start.11 = (bf16[32,1024]{1,0:T(8,128)(2,1)S(1)}, bf16[32,1024]{1,0:T(8,128)(2,1)S(1)}, u32[]{:S(2)}, u32[]{:S(2)}) collective-permute-start(bf16[32,1024]{1,0:T(8,128)(2,1)S(1)} %slice.18), channel_id=1, source_target_pairs={{0,96},{8,104},{16,112},{24,120},{32,0},{40,8},{48,16},{56,24},{64... | collective-permute-start | bytes 196616 | tf_op jit(solution)/shard_map/ppermute | solution.py:33
  86.2 12.3 %collective-permute-start.13 = (bf16[32,1024]{1,0:T(8,128)(2,1)S(1)}, bf16[32,1024]{1,0:T(8,128)(2,1)S(1)}, u32[]{:S(2)}, u32[]{:S(2)}) collective-permute-start(bf16[32,1024]{1,0:T(8,128)(2,1)S(1)} %slice.19), channel_id=1, source_target_pairs={{0,32},{8,40},{16,48},{24,56},{32,64},{40,72},{48,80},{56,88},{64,... | collective-permute-start | bytes 196616 | tf_op jit(solution)/shard_map/ppermute | solution.py:33
  100.4 13.2 %all-to-all-start.3 = ((bf16[4,32,2048]{2,1,0:T(8,128)(2,1)}), bf16[4,32,2048]{2,1,0:T(8,128)(2,1)S(1)}, u32[]{:S(2)}, u32[]{:S(2)}) async-start(bf16[4,32,2048]{2,1,0:T(8,128)(2,1)} %copy.22), calls=%async_computation.3 | async-start | bytes 1048576 | tf_op jit(solution)/shard_map/all_to_all | solution.py:24
  103.9 17.1 %collective-permute-start.7 = (bf16[256,1024]{1,0:T(8,128)(2,1)S(1)}, bf16[256,1024]{1,0:T(8,128)(2,1)}, u32[]{:S(2)}, u32[]{:S(2)}) collective-permute-start(bf16[256,1024]{1,0:T(8,128)(2,1)S(1)} %bitcast.97), channel_id=1, source_target_pairs={{0,6},{2,0},{4,2},{6,4},{1,7},{3,1},{5,3},{7,5},{8,14},{10,8},{12,... | collective-permute-start | bytes 1572872 | tf_op jit(solution)/shard_map/ppermute | solution.py:33
  108.1 15.1 %collective-permute-start.8 = (bf16[256,1024]{1,0:T(8,128)(2,1)S(1)}, bf16[256,1024]{1,0:T(8,128)(2,1)}, u32[]{:S(2)}, u32[]{:S(2)}) collective-permute-start(bf16[256,1024]{1,0:T(8,128)(2,1)S(1)} %bitcast.98), channel_id=1, source_target_pairs={{0,4},{2,6},{4,0},{6,2},{1,5},{3,7},{5,1},{7,3},{8,12},{10,14},{12... | collective-permute-start | bytes 1572872 | tf_op jit(solution)/shard_map/ppermute | solution.py:33
  110.5 26.9 %collective-permute-start.9 = (bf16[256,1024]{1,0:T(8,128)(2,1)S(1)}, bf16[256,1024]{1,0:T(8,128)(2,1)}, u32[]{:S(2)}, u32[]{:S(2)}) collective-permute-start(bf16[256,1024]{1,0:T(8,128)(2,1)S(1)} %bitcast.99), channel_id=1, source_target_pairs={{0,2},{2,4},{4,6},{6,0},{1,3},{3,5},{5,7},{7,1},{8,10},{10,12},{12... | collective-permute-start | bytes 1572872 | tf_op jit(solution)/shard_map/ppermute | solution.py:33
  114.7 30.3 %all-to-all-start.4 = ((f32[8,64,128]{2,1,0:T(8,128)}), f32[8,64,128]{2,1,0:T(8,128)S(1)}, u32[]{:S(2)}, u32[]{:S(2)}) async-start(f32[8,64,128]{2,1,0:T(8,128)} %broadcast_in_dim.44), calls=%async_computation.4 | async-start | bytes 524288 | tf_op jit(solution)/shard_map/all_to_all | solution.py:24
  139.6 4.6 %collective-permute-start.14 = (bf16[4,256,128]{2,1,0:T(8,128)(2,1)S(1)}, bf16[4,256,128]{2,1,0:T(8,128)(2,1)S(1)}, u32[]{:S(2)}, u32[]{:S(2)}) collective-permute-start(bf16[4,256,128]{2,1,0:T(8,128)(2,1)S(1)} %convolution_convert_fusion.3), channel_id=1, source_target_pairs={{0,1},{1,0},{2,3},{3,2},{4,5},{5,4},{6,7},{7,6},{8,9},{9,8},{10,11... | collective-permute-start | bytes 786440 | tf_op jit(solution)/shard_map/ppermute | solution.py:33
  145.0 28.6 %all-to-all-start.1 = ((bf16[16,64,128]{2,1,0:T(8,128)(2,1)}), bf16[16,64,128]{2,1,0:T(8,128)(2,1)S(1)}, u32[]{:S(2)}, u32[]{:S(2)}) async-start(bf16[16,64,128]{2,1,0:T(8,128)(2,1)} %bitcast.25), calls=%async_computation.1 | async-start | bytes 524288 | tf_op jit(solution)/shard_map/all_to_all | solution.py:24

commit v3 on v2

v3 whole, which is shorter than its diff:
```python
import math

import jax
import jax.numpy as jnp
from jax import lax
from jax.experimental import pallas as pl
from jax.experimental.pallas import tpu as pltpu
from jax.sharding import Mesh
from jax.sharding import PartitionSpec as P


VW = 1024
R = 16
K = 8192
L = 64
DP = ("y", "zh", "zl")
MP = ("x", "c")

hash_factor = 73244475
sign_factor = ((hash_factor + (1 << 16)) << 15) % (1 << 32)
sign_factor = sign_factor - (1 << 32) if sign_factor >= (1 << 31) else sign_factor


def swap(parts, axes):
    return lax.all_to_all(parts, axes, split_axis=0, concat_axis=0, tiled=True)


def from_everyone(value, axes):
    return swap(jnp.broadcast_to(value, (lax.axis_size(axes), *value.shape)), axes)


def shifted(value, axes, shift):
    size = lax.axis_size(axes)
    return lax.ppermute(value, axes, [(k, (k + shift) % size) for k in range(size)])


def placed_at(parts, places):
    out = jnp.zeros((len(parts), *parts[0].shape), parts[0].dtype)
    for part, place in zip(parts, places, strict=True):
        out = lax.dynamic_update_slice_in_dim(out, part[None], place, 0)
    return out


def part_of(parts, place):
    return lax.dynamic_index_in_dim(parts, place, 0, keepdims=False)


def sketch_kernel(where, *refs):
    pieces, out, total = refs[:-2], refs[-2], refs[-1]
    seed, first, start = where[0], where[1], where[2]
    depth, width = 2, pieces[0].shape[2]
    cols = out.shape[1]
    shape = (depth * width, 128)
    row = lax.broadcasted_iota(jnp.int32, shape, 0)
    coord = (row // width) * VW + row % width + first
    column = lax.broadcasted_iota(jnp.int32, (1, cols), 1) + start
    low = (column ^ (seed & (K - 1))) * hash_factor
    seed_high = lax.shift_right_logical(seed, 13)

    total[...] = jnp.zeros_like(total)

    def step(k, carry):
        high = (((coord + k * (depth * VW)) ^ seed_high) << 13) * hash_factor
        grads = jnp.concatenate(
            [jnp.concatenate([p[k * depth + d] for p in pieces], axis=0) for d in range(depth)],
            axis=1,
        )
        for t in range(0, cols, 256):
            tiles = []
            for u in range(t, t + 256, 128):
                mixed = high + low[:, u : u + 128]
                mixed = mixed ^ lax.shift_right_logical(mixed, 16)
                mixed = mixed * sign_factor
                tiles.append(jnp.where(mixed < 0, -1.0, 1.0).astype(jnp.bfloat16))
            signs = jnp.concatenate(tiles, axis=1)
            total[:, t : t + 256] += jnp.dot(grads, signs, preferred_element_type=jnp.float32)
        return carry

    lax.fori_loop(0, R // depth, step, 0)
    out[...] = total[...].astype(out.dtype)


def sketched(where, pieces, cols, dtype):
    rows = sum(p.shape[1] for p in pieces)
    flops = 2 * rows * cols * pieces[0].shape[0] * pieces[0].shape[2]
    return pl.pallas_call(
        sketch_kernel,
        out_shape=jax.ShapeDtypeStruct((rows, cols), dtype),
        in_specs=[pl.BlockSpec(memory_space=pltpu.SMEM)]
        + [pl.BlockSpec(memory_space=pltpu.VMEM)] * len(pieces),
        out_specs=pl.BlockSpec(memory_space=pltpu.VMEM),
        scratch_shapes=[pltpu.VMEM((rows, cols), jnp.float32)],
        cost_estimate=pl.CostEstimate(
            flops=flops, bytes_accessed=rows * cols * 4, transcendentals=0
        ),
        compiler_params=pltpu.CompilerParams(vmem_limit_bytes=24 << 20),
        name="sketch",
    )(where, *pieces)


def local_grads(inputs, out_grads):
    return jnp.einsum("ntr,ntj->nrj", inputs, out_grads, preferred_element_type=jnp.float32).astype(
        jnp.bfloat16
    )


def shards(train_in, train_out_grad, query_in, query_out_grad, query_owner, sketch_seed):
    examples, _, width = train_out_grad.shape
    queries = query_in.shape[0]
    ny, nzh, nzl, nx, nc = (lax.axis_size(a) for a in ("y", "zh", "zl", "x", "c"))
    nz = nzh * nzl
    coords_here = R * width

    train_grads = local_grads(train_in, train_out_grad)
    x, y, c, _, zl = (lax.axis_index(a) for a in ("x", "y", "c", "zh", "zl"))
    by_rank = train_grads.swapaxes(0, 1)
    pieces = [by_rank] + [shifted(by_rank, "y", -k) for k in range(1, ny)]

    query_grads = local_grads(query_in, query_out_grad)
    owners = query_owner[:, 0]
    later = lax.broadcasted_iota(jnp.int32, (queries, queries), 0)
    earlier = (owners[:, None] == owners[None, :]) & (
        lax.broadcasted_iota(jnp.int32, (queries, queries), 1) < later
    )
    slot = jnp.sum(earlier.astype(jnp.int32), axis=1)
    capacity = 2
    target = owners * capacity + slot
    placing = (
        lax.broadcasted_iota(jnp.int32, (ny * nz * capacity, queries), 0) == target[None, :]
    ).astype(jnp.bfloat16)
    outgoing = jnp.dot(
        placing, query_grads.reshape(queries, coords_here), preferred_element_type=jnp.float32
    ).astype(jnp.bfloat16)
    arrived = swap(outgoing.reshape(ny * nz, capacity, coords_here), DP)

    half_cols = K // ny // nc
    first = lax.axis_index(MP) * width
    halves = []
    for half, dtype in ((1 - c, jnp.bfloat16), (c, jnp.float32)):
        start = (y * nc + half) * half_cols
        where = jnp.stack([sketch_seed[0], first, start])
        halves.append(sketched(where, pieces, half_cols, dtype))
    traded = shifted(halves[0], "c", 1)
    partial = halves[1] + traded.astype(jnp.float32)
    partial = partial.reshape(ny, examples, half_cols)
    turn = x - y + ny
    features = part_of(partial, lax.rem(turn, ny))
    sent = [
        shifted(part_of(partial, lax.rem(turn + k, ny)).astype(jnp.bfloat16), "x", k)
        for k in range(1, nx)
    ]
    for part in sent:
        features = features + part.astype(jnp.float32)
    feature_scale = 1.0 / math.sqrt(L * R * VW)
    features = (features * feature_scale).astype(jnp.bfloat16)

    near = [features] + [shifted(features, "zl", -k) for k in range(1, nzl)]
    near = placed_at(near, [lax.rem(zl + k, nzl) for k in range(nzl)])
    near = near.reshape(nzl * examples, -1)
    rows = from_everyone(features, "zh").reshape(nc, (nzh // nc) * examples, -1)
    cols = jnp.stack([near] + [shifted(near, "x", -k) for k in range(1, nx)])
    kept, given = (
        jnp.einsum("tmk,nk->tmn", cols, part_of(rows, h), preferred_element_type=jnp.float32)
        for h in (c, 1 - c)
    )
    traded = shifted(given.astype(jnp.bfloat16), "c", 1)
    gram = lax.optimization_barrier(kept) + traded.astype(jnp.float32)
    gram = jnp.stack([part_of(gram, lax.rem(k - x + nx, nx)) for k in range(ny)])
    gram = gram.astype(jnp.bfloat16).reshape(ny * nzl, examples, -1)
    gram = swap(gram, ("y", "zl"))
    gram = gram.reshape(ny, nzl, examples, -1).astype(jnp.float32).sum(axis=0)
    gram = gram * (1.0 / math.sqrt(K))
    gram = gram.reshape(nzl, examples, nzh // nc, examples).transpose(2, 0, 3, 1)
    gram = gram.reshape(-1, examples)

    scores = jnp.einsum(
        "ic,nc->in",
        arrived.reshape(ny * nz * capacity, coords_here),
        train_grads.reshape(examples, coords_here),
        preferred_element_type=jnp.float32,
    )
    score_scale = 1.0 / (L * math.sqrt(R * VW))
    scores = scores.reshape(-1, 2 * examples)
    for axis, size, bit in (("c", nc, 1), ("x", nx, 1), ("x", nx, 2)):
        scores = scores + lax.ppermute(scores, axis, [(k, k ^ bit) for k in range(size)])
    scores = scores * score_scale
    return gram, scores.reshape(1, ny * nz, capacity, examples)


def solution(mesh):
    finer = Mesh(mesh.devices.reshape(4, 4, 4, 4, 2), ("y", "zh", "zl", "x", "c"))
    placed = (
        P(DP, None, None),
        P(DP, None, MP),
        P(DP, None, None),
        P(DP, None, MP),
        P(DP, None),
        P(),
    )
    return jax.shard_map(
        shards,
        mesh=finer,
        in_specs=placed,
        out_specs=(P(MP, DP), P(DP, None, None, None)),
        check_vma=False,
    )
```

time: 176 us -> 171 us (0.972)
  Pallas kernels: 0 us -> 9.18 us
  waiting for transfers between devices: 38.6 us -> 46.7 us
  other arithmetic: 10 us -> 2.37 us
  starting transfers between devices: 102 us -> 95.7 us
  matrix products: 14.1 us -> 7.9 us
  local copies, waits for them, and re-layouts: 8.19 us -> 5.71 us
    all_to_all x5 -> x3, starting transfers between devices: 47.9 us -> 38.6 us  [swap(): return lax.all_to_all(parts, axes, split_axis=0, concat_axis=0, tiled=True)]
    pallas_call x0 -> x2, Pallas kernels: none -> 9.18 us  [sketched(): pl.pallas_call(sketch_kernel, out_shape=jax.ShapeDtypeStruct((rows, cols)...]
    ppermute x0 -> x3, starting transfers between devices: none -> 8.96 us  [shards(): lax.ppermute(scores, axis, [(k, k ^ bit) for k in range(size)])]
    ppermute x15 -> x14, starting transfers between devices: 54.3 us -> 48.2 us  [shifted(): lax.ppermute(value, axes, [(k, (k + shift) % size) for k in range(size)])]
    ppermute x0 -> x3, waiting for transfers between devices: none -> 5.21 us  [shards(): lax.ppermute(scores, axis, [(k, k ^ bit) for k in range(size)])]
    convert_element_type x1 -> x0, other arithmetic: 5.09 us -> none  [sign_table(): return jnp.where(mixed < 0, -1.0, 1.0).astype(jnp.bfloat16)]
    dot_general x4 -> x2, matrix products: 9.73 us -> 4.69 us  [shards(): jnp.einsum('tmk,nk->tmn', cols, part_of(rows, h), preferred_element_type=...]
    ppermute x15 -> x14, waiting for transfers between devices: 29.3 us -> 30.9 us  [shifted(): lax.ppermute(value, axes, [(k, (k + shift) % size) for k in range(size)])]
  transfers between devices with their start and end apart: 20 -> 20, of which waited for: 9 -> 10; matrix products, arithmetic and copies ran while one was open for 15% -> 6% of each run, Pallas kernels for 0% -> 3%
where the time goes in v3:
time: 171 us; the launch traced here: 169 us
  starting transfers between devices  95.7 us (56%)
  waiting for transfers between devices  46.7 us (27%)
  Pallas kernels  9.18 us (5%)
  matrix products  7.9 us (5%)
  local copies, waits for them, and re-layouts  5.71 us (3%)
  other arithmetic  2.37 us (1%)
  between operations  1.77 us (1%)
    ppermute x14, starting transfers between devices, shifted(): lax.ppermute(value, axes, [(k, (k + shift) % size) for k in range(size)])  48.2 us
    all_to_all x3, starting transfers between devices, swap(): return lax.all_to_all(parts, axes, split_axis=0, concat_axis=0, tiled=True)  38.6 us
    ppermute x14, waiting for transfers between devices, shifted(): lax.ppermute(value, axes, [(k, (k + shift) % size) for k in range(size)])  30.9 us
    all_to_all x3, waiting for transfers between devices, swap(): return lax.all_to_all(parts, axes, split_axis=0, concat_axis=0, tiled=True)  10.5 us
    pallas_call x2, Pallas kernels, sketched(): pl.pallas_call(sketch_kernel, out_shape=jax.ShapeDtypeStruct((rows, cols)...  9.18 us
    ppermute x3, starting transfers between devices, shards(): lax.ppermute(scores, axis, [(k, k ^ bit) for k in range(size)])  8.96 us
    ppermute x3, waiting for transfers between devices, shards(): lax.ppermute(scores, axis, [(k, k ^ bit) for k in range(size)])  5.21 us
    dot_general x2, matrix products, shards(): jnp.einsum('tmk,nk->tmn', cols, part_of(rows, h), preferred_element_type=...  4.69 us
  transfers between devices with their start and end apart: 20, of which 10 were waited for; matrix products, arithmetic and copies ran while one was open for 6% of the time, Pallas kernels for 3%

profile of v3, /device:TPU:1, one launch (start us, length us, event | category | flops | bytes accessed | tf_op | source)
XLA Modules:
  0.0 169.3 jit_solution(7216409945411906334)
XLA Ops:
  3.3 4.0 %collective-permute-start.2 = (bf16[16,64,128]{2,1,0:T(8,128)(2,1)S(1)}, bf16[16,64,128]{2,1,0:T(8,128)(2,1)S(1)}, u32[]{:S(2)}, u32[]{:S(2)}) collective-permute-start(bf16[16,64,128]{2,1,0:T(8,128)(2,1)S(1)} %bitcast.68), channel_id=1, source_target_pairs={{0,128},{128,256},{256,384},{384,0},{1,129},{129,257},{257,385},{3... | collective-permute-start | bytes 786440 | tf_op jit(solution)/shard_map/ppermute | solution.py:34
  7.3 4.5 %collective-permute-start.1 = (bf16[16,64,128]{2,1,0:T(8,128)(2,1)S(1)}, bf16[16,64,128]{2,1,0:T(8,128)(2,1)S(1)}, u32[]{:S(2)}, u32[]{:S(2)}) collective-permute-start(bf16[16,64,128]{2,1,0:T(8,128)(2,1)S(1)} %bitcast.69), channel_id=1, source_target_pairs={{0,256},{128,384},{256,0},{384,128},{1,257},{129,385},{257,1},{385... | collective-permute-start | bytes 786440 | tf_op jit(solution)/shard_map/ppermute | solution.py:34
  11.8 3.0 %collective-permute-start = (bf16[16,64,128]{2,1,0:T(8,128)(2,1)S(1)}, bf16[16,64,128]{2,1,0:T(8,128)(2,1)S(1)}, u32[]{:S(2)}, u32[]{:S(2)}) collective-permute-start(bf16[16,64,128]{2,1,0:T(8,128)(2,1)S(1)} %bitcast.70), channel_id=1, source_target_pairs={{0,384},{128,0},{256,128},{384,256},{1,385},{129,1},{257,129},{385... | collective-permute-start | bytes 786440 | tf_op jit(solution)/shard_map/ppermute | solution.py:34
  15.6 5.0 %collective-permute-done.1.refs_2_ = bf16[16,64,128]{2,1,0:T(8,128)(2,1)S(1)} collective-permute-done((bf16[16,64,128]{2,1,0:T(8,128)(2,1)S(1)}, bf16[16,64,128]{2,1,0:T(8,128)(2,1)S(1)}, u32[]{:S(2)}, u32[]{:S(2)}) %collective-permute-start.1) | collective-permute-done | bytes 262176 | tf_op jit(solution)/shard_map/ppermute | solution.py:34
  20.6 4.6 %sketch.3 = bf16[256,1024]{1,0:T(8,128)(2,1)S(1)} custom-call(s32[3]{0:T(128)S(1)} %pad_add_fusion.2.where, bf16[16,64,128]{2,1,0:T(8,128)(2,1)S(1)} %bitcast.71, bf16[16,64,128]{2,1,0:T(8,128)(2,1)S(1)} %collective-permute-done.refs_1_, bf16[16,64,128]{2,1,0:T(8,128)(2,1)S(1)} %collective-permute-done.1.refs_2_, ...), custom_call_target="tpu_custom_call" | custom-call | flops 1073741824 | bytes 1048576 | tf_op jit(solution)/shard_map/sketch/pallas_call | solution.py:86
  25.2 6.6 %collective-permute-start.3 = (bf16[256,1024]{1,0:T(8,128)(2,1)S(1)}, bf16[256,1024]{1,0:T(8,128)(2,1)S(1)}, u32[]{:S(2)}, u32[]{:S(2)}) collective-permute-start(bf16[256,1024]{1,0:T(8,128)(2,1)S(1)} %sketch.3), channel_id=1, source_target_pairs={{0,1},{1,0},{2,3},{3,2},{4,5},{5,4},{6,7},{7,6},{8,9},{9,8},{10,11... | collective-permute-start | bytes 1572872 | tf_op jit(solution)/shard_map/ppermute | solution.py:34
  31.9 4.6 %sketch.2 = f32[256,1024]{1,0:T(8,128)S(1)} custom-call(s32[3]{0:T(128)S(1)} %pad_add_fusion.where, bf16[16,64,128]{2,1,0:T(8,128)(2,1)S(1)} %bitcast.72, bf16[16,64,128]{2,1,0:T(8,128)(2,1)S(1)} %collective-permute-done.refs_1_, bf16[16,64,128]{2,1,0:T(8,128)(2,1)S(1)} %collective-permute-done.1.refs_2_, bf16[16,64,128]{2,1,0:T(8,128)(2,1)S(1)} %collective-permute-done.2.refs_3_), custom_call_target="tpu_custom_call" | custom-call | flops 1073741824 | bytes 1048576 | tf_op jit(solution)/shard_map/sketch/pallas_call | solution.py:86
  36.7 2.0 %collective-permute-start.4 = (bf16[64,1024]{1,0:T(8,128)(2,1)S(1)}, bf16[64,1024]{1,0:T(8,128)(2,1)S(1)}, u32[]{:S(2)}, u32[]{:S(2)}) collective-permute-start(bf16[64,1024]{1,0:T(8,128)(2,1)S(1)} %get-tuple-element.4), channel_id=1, source_target_pairs={{0,2},{2,4},{4,6},{6,0},{1,3},{3,5},{5,7},{7,1},{8,10},{10,12},{12... | collective-permute-start | bytes 393224 | tf_op jit(solution)/shard_map/ppermute | solution.py:34
  38.7 4.5 %collective-permute-start.6 = (bf16[64,1024]{1,0:T(8,128)(2,1)S(1)}, bf16[64,1024]{1,0:T(8,128)(2,1)S(1)}, u32[]{:S(2)}, u32[]{:S(2)}) collective-permute-start(bf16[64,1024]{1,0:T(8,128)(2,1)S(1)} %get-tuple-element.5), channel_id=1, source_target_pairs={{0,6},{2,0},{4,2},{6,4},{1,7},{3,1},{5,3},{7,5},{8,14},{10,8},{12,... | collective-permute-start | bytes 393224 | tf_op jit(solution)/shard_map/ppermute | solution.py:34
  43.2 2.3 %collective-permute-start.5 = (bf16[64,1024]{1,0:T(8,128)(2,1)S(1)}, bf16[64,1024]{1,0:T(8,128)(2,1)S(1)}, u32[]{:S(2)}, u32[]{:S(2)}) collective-permute-start(bf16[64,1024]{1,0:T(8,128)(2,1)S(1)} %get-tuple-element.6), channel_id=1, source_target_pairs={{0,4},{2,6},{4,0},{6,2},{1,5},{3,7},{5,1},{7,3},{8,12},{10,14},{12... | collective-permute-start | bytes 393224 | tf_op jit(solution)/shard_map/ppermute | solution.py:34
  45.8 5.3 %collective-permute-done.5 = bf16[64,1024]{1,0:T(8,128)(2,1)S(1)} collective-permute-done((bf16[64,1024]{1,0:T(8,128)(2,1)S(1)}, bf16[64,1024]{1,0:T(8,128)(2,1)S(1)}, u32[]{:S(2)}, u32[]{:S(2)}) %collective-permute-start.5) | collective-permute-done | bytes 131104 | tf_op jit(solution)/shard_map/ppermute | solution.py:34
  52.1 13.6 %all-to-all-start = ((bf16[4,64,1024]{2,1,0:T(8,128)(2,1)}), bf16[4,64,1024]{2,1,0:T(8,128)(2,1)S(1)}, u32[]{:S(2)}, u32[]{:S(2)}) async-start(bf16[4,64,1024]{2,1,0:T(8,128)(2,1)} %broadcast_in_dim.24), calls=%async_computation | async-start | bytes 1048576 | tf_op jit(solution)/shard_map/all_to_all | solution.py:25
  67.3 3.6 %collective-permute-start.7 = (bf16[64,1024]{1,0:T(8,128)(2,1)S(1)}, bf16[64,1024]{1,0:T(8,128)(2,1)S(1)}, u32[]{:S(2)}, u32[]{:S(2)}) collective-permute-start(bf16[64,1024]{1,0:T(8,128)(2,1)S(1)} %get-tuple-element.3), channel_id=1, source_target_pairs={{0,24},{8,0},{16,8},{24,16},{1,25},{9,1},{17,9},{25,17},{2,26},{10... | collective-permute-start | bytes 393224 | tf_op jit(solution)/shard_map/ppermute | solution.py:34
  72.3 1.9 %collective-permute-start.9 = (bf16[64,1024]{1,0:T(8,128)(2,1)S(1)}, bf16[64,1024]{1,0:T(8,128)(2,1)S(1)}, u32[]{:S(2)}, u32[]{:S(2)}) collective-permute-start(bf16[64,1024]{1,0:T(8,128)(2,1)S(1)} %get-tuple-element.3), channel_id=1, source_target_pairs={{0,8},{8,16},{16,24},{24,0},{1,9},{9,17},{17,25},{25,1},{2,10},{10... | collective-permute-start | bytes 393224 | tf_op jit(solution)/shard_map/ppermute | solution.py:34
  74.2 2.9 %collective-permute-start.8 = (bf16[64,1024]{1,0:T(8,128)(2,1)S(1)}, bf16[64,1024]{1,0:T(8,128)(2,1)S(1)}, u32[]{:S(2)}, u32[]{:S(2)}) collective-permute-start(bf16[64,1024]{1,0:T(8,128)(2,1)S(1)} %get-tuple-element.3), channel_id=1, source_target_pairs={{0,16},{8,24},{16,0},{24,8},{1,17},{9,25},{17,1},{25,9},{2,18},{10... | collective-permute-start | bytes 393224 | tf_op jit(solution)/shard_map/ppermute | solution.py:34
  77.2 10.5 %all-to-all-done = bf16[4,64,1024]{2,1,0:T(8,128)(2,1)S(1)} async-done(((bf16[4,64,1024]{2,1,0:T(8,128)(2,1)}), bf16[4,64,1024]{2,1,0:T(8,128)(2,1)S(1)}, u32[]{:S(2)}, u32[]{:S(2)}) %all-to-all-start) | async-done | bytes 524320 | tf_op jit(solution)/shard_map/all_to_all | solution.py:25
  87.7 18.2 %all-to-all-start.2 = ((bf16[64,2,2048]{2,1,0:T(2,128)(2,1)}), bf16[64,2,2048]{2,1,0:T(2,128)(2,1)S(1)}, u32[]{:S(2)}, u32[]{:S(2)}) async-start(bf16[64,2,2048]{2,1,0:T(2,128)(2,1)} %reshape.61), calls=%async_computation.2 | async-start | bytes 1048576 | tf_op jit(solution)/shard_map/all_to_all | solution.py:25
  106.0 1.9 %collective-permute-start.12 = (bf16[256,1024]{1,0:T(8,128)(2,1)S(1)}, bf16[256,1024]{1,0:T(8,128)(2,1)S(1)}, u32[]{:S(2)}, u32[]{:S(2)}) collective-permute-start(bf16[256,1024]{1,0:T(8,128)(2,1)S(1)} %bitcast.79), channel_id=1, source_target_pairs={{0,2},{2,4},{4,6},{6,0},{1,3},{3,5},{5,7},{7,1},{8,10},{10,12},{12... | collective-permute-start | bytes 1572872 | tf_op jit(solution)/shard_map/ppermute | solution.py:34
  108.0 4.3 %collective-permute-start.11 = (bf16[256,1024]{1,0:T(8,128)(2,1)S(1)}, bf16[256,1024]{1,0:T(8,128)(2,1)}, u32[]{:S(2)}, u32[]{:S(2)}) collective-permute-start(bf16[256,1024]{1,0:T(8,128)(2,1)S(1)} %bitcast.80), channel_id=1, source_target_pairs={{0,4},{2,6},{4,0},{6,2},{1,5},{3,7},{5,1},{7,3},{8,12},{10,14},{12... | collective-permute-start | bytes 1572872 | tf_op jit(solution)/shard_map/ppermute | solution.py:34
  112.3 3.1 %collective-permute-start.10 = (bf16[256,1024]{1,0:T(8,128)(2,1)S(1)}, bf16[256,1024]{1,0:T(8,128)(2,1)}, u32[]{:S(2)}, u32[]{:S(2)}) collective-permute-start(bf16[256,1024]{1,0:T(8,128)(2,1)S(1)} %bitcast.81), channel_id=1, source_target_pairs={{0,6},{2,0},{4,2},{6,4},{1,7},{3,1},{5,3},{7,5},{8,14},{10,8},{12,... | collective-permute-start | bytes 1572872 | tf_op jit(solution)/shard_map/ppermute | solution.py:34
  115.4 5.3 %collective-permute-done.12 = bf16[256,1024]{1,0:T(8,128)(2,1)S(1)} collective-permute-done((bf16[256,1024]{1,0:T(8,128)(2,1)S(1)}, bf16[256,1024]{1,0:T(8,128)(2,1)S(1)}, u32[]{:S(2)}, u32[]{:S(2)}) %collective-permute-start.12) | collective-permute-done | bytes 524320 | tf_op jit(solution)/shard_map/ppermute | solution.py:34
  120.7 11.0 %collective-permute-done.11 = bf16[256,1024]{1,0:T(8,128)(2,1)} collective-permute-done((bf16[256,1024]{1,0:T(8,128)(2,1)S(1)}, bf16[256,1024]{1,0:T(8,128)(2,1)}, u32[]{:S(2)}, u32[]{:S(2)}) %collective-permute-start.11) | collective-permute-done | bytes 524320 | tf_op jit(solution)/shard_map/ppermute | solution.py:34
  131.7 4.0 %collective-permute-done.10 = bf16[256,1024]{1,0:T(8,128)(2,1)} collective-permute-done((bf16[256,1024]{1,0:T(8,128)(2,1)S(1)}, bf16[256,1024]{1,0:T(8,128)(2,1)}, u32[]{:S(2)}, u32[]{:S(2)}) %collective-permute-start.10) | collective-permute-done | bytes 524320 | tf_op jit(solution)/shard_map/ppermute | solution.py:34
  135.7 2.6 %convolution_convert_fusion.2 = bf16[4,256,128]{2,1,0:T(8,128)(2,1)} fusion(bf16[1,256,1024]{2,1,0:T(8,128)(2,1)S(1)} %bitcast.86, bf16[1,256,1024]{2,1,0:T(8,128)(2,1)} %bitcast.16, bf16[1,256,1024]{2,1,0:T(8,128)(2,1)} %bitcast.15, bf16[1,256,1024]{2,1,0:T(8,128)(2,1)S(1)} %bitcast.82, bf16[2,128,1024]{2,1,0:T(8,128)(2,1)S(1)} %bitcast.84, s32[]{:T(128)S(6)} %select_n.54), kind=kOutput, calls=%fused_computation.3 | convolution fusion | flops 271712256 | bytes 2621444 | tf_op jit(solution)/shard_map/tmk,nk->tmn/dot_general | solution.py:163
  138.3 3.6 %collective-permute-start.13 = (bf16[4,256,128]{2,1,0:T(8,128)(2,1)}, bf16[4,256,128]{2,1,0:T(8,128)(2,1)}, u32[]{:S(2)}, u32[]{:S(2)}) collective-permute-start(bf16[4,256,128]{2,1,0:T(8,128)(2,1)} %convolution_convert_fusion.2), channel_id=1, source_target_pairs={{0,1},{1,0},{2,3},{3,2},{4,5},{5,4},{6,7},{7,6},{8,9},{9,8},{10,11... | collective-permute-start | bytes 786440 | tf_op jit(solution)/shard_map/ppermute | solution.py:34
  141.9 2.1 %fusion = f32[4,256,128]{2,1,0:T(8,128)S(1)} fusion(bf16[1,256,1024]{2,1,0:T(8,128)(2,1)} %bitcast.87, bf16[1,256,1024]{2,1,0:T(8,128)(2,1)} %bitcast.16, bf16[1,256,1024]{2,1,0:T(8,128)(2,1)} %bitcast.15, bf16[1,256,1024]{2,1,0:T(8,128)(2,1)S(1)} %bitcast.83, bf16[2,128,1024]{2,1,0:T(8,128)(2,1)S(1)} %bitcast.85, s32[]{:T(128)S(6)} %select_n.53), kind=kOutput, calls=%fused_computation.8 | convolution fusion | flops 271581184 | bytes 2883588 | tf_op jit(solution)/shard_map/tmk,nk->tmn/dot_general | solution.py:163
  145.8 6.7 %all-to-all-start.1 = ((bf16[16,64,128]{2,1,0:T(8,128)(2,1)}), bf16[16,64,128]{2,1,0:T(8,128)(2,1)S(1)}, u32[]{:S(2)}, u32[]{:S(2)}) async-start(bf16[16,64,128]{2,1,0:T(8,128)(2,1)} %bitcast.23), calls=%async_computation.1 | async-start | bytes 524288 | tf_op jit(solution)/shard_map/all_to_all | solution.py:25
  153.1 2.2 %collective-permute-start.14 = (f32[64,128]{1,0:T(8,128)S(1)}, f32[64,128]{1,0:T(8,128)S(1)}, u32[]{:S(2)}, u32[]{:S(2)}) collective-permute-start(f32[64,128]{1,0:T(8,128)S(1)} %reshape.64), channel_id=1, source_target_pairs={{0,1},{1,0},{2,3},{3,2},{4,5},{5,4},{6,7},{7,6},{8,9},{9,8},{10,11... | collective-permute-start | bytes 98312 | tf_op jit(solution)/shard_map/ppermute | solution.py:185
  156.2 2.8 %collective-permute-start.15 = (f32[64,128]{1,0:T(8,128)S(1)}, f32[64,128]{1,0:T(8,128)S(1)}, u32[]{:S(2)}, u32[]{:S(2)}) collective-permute-start(f32[64,128]{1,0:T(8,128)S(1)} %add.163), channel_id=1, source_target_pairs={{0,2},{2,0},{4,6},{6,4},{1,3},{3,1},{5,7},{7,5},{8,10},{10,8},{12,... | collective-permute-start | bytes 98312 | tf_op jit(solution)/shard_map/ppermute | solution.py:185
  159.0 2.1 %collective-permute-done.15 = f32[64,128]{1,0:T(8,128)S(1)} collective-permute-done((f32[64,128]{1,0:T(8,128)S(1)}, f32[64,128]{1,0:T(8,128)S(1)}, u32[]{:S(2)}, u32[]{:S(2)}) %collective-permute-start.15) | collective-permute-done | bytes 32800 | tf_op jit(solution)/shard_map/ppermute | solution.py:185
  161.1 4.0 %collective-permute-start.16 = (f32[64,128]{1,0:T(8,128)S(1)}, f32[64,128]{1,0:T(8,128)S(1)}, u32[]{:S(2)}, u32[]{:S(2)}) collective-permute-start(f32[64,128]{1,0:T(8,128)S(1)} %add.164), channel_id=1, source_target_pairs={{0,4},{2,6},{4,0},{6,2},{1,5},{3,7},{5,1},{7,3},{8,12},{10,14},{12... | collective-permute-start | bytes 98312 | tf_op jit(solution)/shard_map/ppermute | solution.py:185
  165.1 2.2 %collective-permute-done.16 = f32[64,128]{1,0:T(8,128)S(1)} collective-permute-done((f32[64,128]{1,0:T(8,128)S(1)}, f32[64,128]{1,0:T(8,128)S(1)}, u32[]{:S(2)}, u32[]{:S(2)}) %collective-permute-start.16) | collective-permute-done | bytes 32800 | tf_op jit(solution)/shard_map/ppermute | solution.py:185
  (52 shorter events, 12.4 us)
Async XLA Ops:
  0.6 1.2 copy-start
  3.3 12.3 %collective-permute-start.2 = (bf16[16,64,128]{2,1,0:T(8,128)(2,1)S(1)}, bf16[16,64,128]{2,1,0:T(8,128)(2,1)S(1)}, u32[]{:S(2)}, u32[]{:S(2)}) collective-permute-start(bf16[16,64,128]{2,1,0:T(8,128)(2,1)S(1)} %bitcast.68), channel_id=1, source_target_pairs={{0,128},{128,256},{256,384},{384,0},{1,129},{129,257},{257,385},{3... | collective-permute-start | bytes 786440 | tf_op jit(solution)/shard_map/ppermute | solution.py:34
  7.3 13.3 %collective-permute-start.1 = (bf16[16,64,128]{2,1,0:T(8,128)(2,1)S(1)}, bf16[16,64,128]{2,1,0:T(8,128)(2,1)S(1)}, u32[]{:S(2)}, u32[]{:S(2)}) collective-permute-start(bf16[16,64,128]{2,1,0:T(8,128)(2,1)S(1)} %bitcast.69), channel_id=1, source_target_pairs={{0,256},{128,384},{256,0},{384,128},{1,257},{129,385},{257,1},{385... | collective-permute-start | bytes 786440 | tf_op jit(solution)/shard_map/ppermute | solution.py:34
  11.8 8.7 %collective-permute-start = (bf16[16,64,128]{2,1,0:T(8,128)(2,1)S(1)}, bf16[16,64,128]{2,1,0:T(8,128)(2,1)S(1)}, u32[]{:S(2)}, u32[]{:S(2)}) collective-permute-start(bf16[16,64,128]{2,1,0:T(8,128)(2,1)S(1)} %bitcast.70), channel_id=1, source_target_pairs={{0,384},{128,0},{256,128},{384,256},{1,385},{129,1},{257,129},{385... | collective-permute-start | bytes 786440 | tf_op jit(solution)/shard_map/ppermute | solution.py:34
  25.2 11.3 %collective-permute-start.3 = (bf16[256,1024]{1,0:T(8,128)(2,1)S(1)}, bf16[256,1024]{1,0:T(8,128)(2,1)S(1)}, u32[]{:S(2)}, u32[]{:S(2)}) collective-permute-start(bf16[256,1024]{1,0:T(8,128)(2,1)S(1)} %sketch.3), channel_id=1, source_target_pairs={{0,1},{1,0},{2,3},{3,2},{4,5},{5,4},{6,7},{7,6},{8,9},{9,8},{10,11... | collective-permute-start | bytes 1572872 | tf_op jit(solution)/shard_map/ppermute | solution.py:34
  36.7 8.8 %collective-permute-start.4 = (bf16[64,1024]{1,0:T(8,128)(2,1)S(1)}, bf16[64,1024]{1,0:T(8,128)(2,1)S(1)}, u32[]{:S(2)}, u32[]{:S(2)}) collective-permute-start(bf16[64,1024]{1,0:T(8,128)(2,1)S(1)} %get-tuple-element.4), channel_id=1, source_target_pairs={{0,2},{2,4},{4,6},{6,0},{1,3},{3,5},{5,7},{7,1},{8,10},{10,12},{12... | collective-permute-start | bytes 393224 | tf_op jit(solution)/shard_map/ppermute | solution.py:34
  38.7 7.1 %collective-permute-start.6 = (bf16[64,1024]{1,0:T(8,128)(2,1)S(1)}, bf16[64,1024]{1,0:T(8,128)(2,1)S(1)}, u32[]{:S(2)}, u32[]{:S(2)}) collective-permute-start(bf16[64,1024]{1,0:T(8,128)(2,1)S(1)} %get-tuple-element.5), channel_id=1, source_target_pairs={{0,6},{2,0},{4,2},{6,4},{1,7},{3,1},{5,3},{7,5},{8,14},{10,8},{12,... | collective-permute-start | bytes 393224 | tf_op jit(solution)/shard_map/ppermute | solution.py:34
  43.2 7.9 %collective-permute-start.5 = (bf16[64,1024]{1,0:T(8,128)(2,1)S(1)}, bf16[64,1024]{1,0:T(8,128)(2,1)S(1)}, u32[]{:S(2)}, u32[]{:S(2)}) collective-permute-start(bf16[64,1024]{1,0:T(8,128)(2,1)S(1)} %get-tuple-element.6), channel_id=1, source_target_pairs={{0,4},{2,6},{4,0},{6,2},{1,5},{3,7},{5,1},{7,3},{8,12},{10,14},{12... | collective-permute-start | bytes 393224 | tf_op jit(solution)/shard_map/ppermute | solution.py:34
  51.2 14.5 %copy-start.3 = (s32[64,1]{0,1:T(1,128)S(1)}, s32[64,1]{0,1:T(1,128)}, u32[]{:S(2)}) copy-start(s32[64,1]{0,1:T(1,128)} %param.10) | copy-start | bytes 772
  51.3 14.7 %copy-start.1 = (bf16[64,64,128]{2,1,0:T(8,128)(2,1)S(1)}, bf16[64,64,128]{2,1,0:T(8,128)(2,1)}, u32[]{:S(2)}) copy-start(bf16[64,64,128]{2,1,0:T(8,128)(2,1)} %param.9) | copy-start | bytes 3145732
  52.1 35.6 %all-to-all-start = ((bf16[4,64,1024]{2,1,0:T(8,128)(2,1)}), bf16[4,64,1024]{2,1,0:T(8,128)(2,1)S(1)}, u32[]{:S(2)}, u32[]{:S(2)}) async-start(bf16[4,64,1024]{2,1,0:T(8,128)(2,1)} %broadcast_in_dim.24), calls=%async_computation | async-start | bytes 1048576 | tf_op jit(solution)/shard_map/all_to_all | solution.py:25
  67.3 38.6 %collective-permute-start.7 = (bf16[64,1024]{1,0:T(8,128)(2,1)S(1)}, bf16[64,1024]{1,0:T(8,128)(2,1)S(1)}, u32[]{:S(2)}, u32[]{:S(2)}) collective-permute-start(bf16[64,1024]{1,0:T(8,128)(2,1)S(1)} %get-tuple-element.3), channel_id=1, source_target_pairs={{0,24},{8,0},{16,8},{24,16},{1,25},{9,1},{17,9},{25,17},{2,26},{10... | collective-permute-start | bytes 393224 | tf_op jit(solution)/shard_map/ppermute | solution.py:34
  72.3 33.7 %collective-permute-start.9 = (bf16[64,1024]{1,0:T(8,128)(2,1)S(1)}, bf16[64,1024]{1,0:T(8,128)(2,1)S(1)}, u32[]{:S(2)}, u32[]{:S(2)}) collective-permute-start(bf16[64,1024]{1,0:T(8,128)(2,1)S(1)} %get-tuple-element.3), channel_id=1, source_target_pairs={{0,8},{8,16},{16,24},{24,0},{1,9},{9,17},{17,25},{25,1},{2,10},{10... | collective-permute-start | bytes 393224 | tf_op jit(solution)/shard_map/ppermute | solution.py:34
  74.2 31.7 %collective-permute-start.8 = (bf16[64,1024]{1,0:T(8,128)(2,1)S(1)}, bf16[64,1024]{1,0:T(8,128)(2,1)S(1)}, u32[]{:S(2)}, u32[]{:S(2)}) collective-permute-start(bf16[64,1024]{1,0:T(8,128)(2,1)S(1)} %get-tuple-element.3), channel_id=1, source_target_pairs={{0,16},{8,24},{16,0},{24,8},{1,17},{9,25},{17,1},{25,9},{2,18},{10... | collective-permute-start | bytes 393224 | tf_op jit(solution)/shard_map/ppermute | solution.py:34
  87.7 58.1 %all-to-all-start.2 = ((bf16[64,2,2048]{2,1,0:T(2,128)(2,1)}), bf16[64,2,2048]{2,1,0:T(2,128)(2,1)S(1)}, u32[]{:S(2)}, u32[]{:S(2)}) async-start(bf16[64,2,2048]{2,1,0:T(2,128)(2,1)} %reshape.61), calls=%async_computation.2 | async-start | bytes 1048576 | tf_op jit(solution)/shard_map/all_to_all | solution.py:25
  106.0 14.7 %collective-permute-start.12 = (bf16[256,1024]{1,0:T(8,128)(2,1)S(1)}, bf16[256,1024]{1,0:T(8,128)(2,1)S(1)}, u32[]{:S(2)}, u32[]{:S(2)}) collective-permute-start(bf16[256,1024]{1,0:T(8,128)(2,1)S(1)} %bitcast.79), channel_id=1, source_target_pairs={{0,2},{2,4},{4,6},{6,0},{1,3},{3,5},{5,7},{7,1},{8,10},{10,12},{12... | collective-permute-start | bytes 1572872 | tf_op jit(solution)/shard_map/ppermute | solution.py:34
  108.0 23.8 %collective-permute-start.11 = (bf16[256,1024]{1,0:T(8,128)(2,1)S(1)}, bf16[256,1024]{1,0:T(8,128)(2,1)}, u32[]{:S(2)}, u32[]{:S(2)}) collective-permute-start(bf16[256,1024]{1,0:T(8,128)(2,1)S(1)} %bitcast.80), channel_id=1, source_target_pairs={{0,4},{2,6},{4,0},{6,2},{1,5},{3,7},{5,1},{7,3},{8,12},{10,14},{12... | collective-permute-start | bytes 1572872 | tf_op jit(solution)/shard_map/ppermute | solution.py:34
  112.3 23.4 %collective-permute-start.10 = (bf16[256,1024]{1,0:T(8,128)(2,1)S(1)}, bf16[256,1024]{1,0:T(8,128)(2,1)}, u32[]{:S(2)}, u32[]{:S(2)}) collective-permute-start(bf16[256,1024]{1,0:T(8,128)(2,1)S(1)} %bitcast.81), channel_id=1, source_target_pairs={{0,6},{2,0},{4,2},{6,4},{1,7},{3,1},{5,3},{7,5},{8,14},{10,8},{12,... | collective-permute-start | bytes 1572872 | tf_op jit(solution)/shard_map/ppermute | solution.py:34
  120.7 17.6 %copy-start.2 = (bf16[256,1024]{1,0:T(8,128)(2,1)}, bf16[256,1024]{1,0:T(8,128)(2,1)S(1)}, u32[]{:S(2)}) copy-start(bf16[256,1024]{1,0:T(8,128)(2,1)S(1)} %collective-permute-done.12) | copy-start | bytes 1572868
  138.3 5.7 %collective-permute-start.13 = (bf16[4,256,128]{2,1,0:T(8,128)(2,1)}, bf16[4,256,128]{2,1,0:T(8,128)(2,1)}, u32[]{:S(2)}, u32[]{:S(2)}) collective-permute-start(bf16[4,256,128]{2,1,0:T(8,128)(2,1)} %convolution_convert_fusion.2), channel_id=1, source_target_pairs={{0,1},{1,0},{2,3},{3,2},{4,5},{5,4},{6,7},{7,6},{8,9},{9,8},{10,11... | collective-permute-start | bytes 786440 | tf_op jit(solution)/shard_map/ppermute | solution.py:34
  145.8 22.2 %all-to-all-start.1 = ((bf16[16,64,128]{2,1,0:T(8,128)(2,1)}), bf16[16,64,128]{2,1,0:T(8,128)(2,1)S(1)}, u32[]{:S(2)}, u32[]{:S(2)}) async-start(bf16[16,64,128]{2,1,0:T(8,128)(2,1)} %bitcast.23), calls=%async_computation.1 | async-start | bytes 524288 | tf_op jit(solution)/shard_map/all_to_all | solution.py:25
  153.1 3.1 %collective-permute-start.14 = (f32[64,128]{1,0:T(8,128)S(1)}, f32[64,128]{1,0:T(8,128)S(1)}, u32[]{:S(2)}, u32[]{:S(2)}) collective-permute-start(f32[64,128]{1,0:T(8,128)S(1)} %reshape.64), channel_id=1, source_target_pairs={{0,1},{1,0},{2,3},{3,2},{4,5},{5,4},{6,7},{7,6},{8,9},{9,8},{10,11... | collective-permute-start | bytes 98312 | tf_op jit(solution)/shard_map/ppermute | solution.py:185
  156.2 4.9 %collective-permute-start.15 = (f32[64,128]{1,0:T(8,128)S(1)}, f32[64,128]{1,0:T(8,128)S(1)}, u32[]{:S(2)}, u32[]{:S(2)}) collective-permute-start(f32[64,128]{1,0:T(8,128)S(1)} %add.163), channel_id=1, source_target_pairs={{0,2},{2,0},{4,6},{6,4},{1,3},{3,1},{5,7},{7,5},{8,10},{10,8},{12,... | collective-permute-start | bytes 98312 | tf_op jit(solution)/shard_map/ppermute | solution.py:185
  161.1 6.2 %collective-permute-start.16 = (f32[64,128]{1,0:T(8,128)S(1)}, f32[64,128]{1,0:T(8,128)S(1)}, u32[]{:S(2)}, u32[]{:S(2)}) collective-permute-start(f32[64,128]{1,0:T(8,128)S(1)} %add.164), channel_id=1, source_target_pairs={{0,4},{2,6},{4,0},{6,2},{1,5},{3,7},{5,1},{7,3},{8,12},{10,14},{12... | collective-permute-start | bytes 98312 | tf_op jit(solution)/shard_map/ppermute | solution.py:185

commit v4 on v3

--- a/solution.py
+++ b/solution.py
@@ -76,7 +76,7 @@
             total[:, t : t + 256] += jnp.dot(grads, signs, preferred_element_type=jnp.float32)
         return carry
 
-    lax.fori_loop(0, R // depth, step, 0)
+    lax.fori_loop(0, R // depth, step, 0, unroll=True)
     out[...] = total[...].astype(out.dtype)
 
 
@@ -141,14 +141,14 @@
         where = jnp.stack([sketch_seed[0], first, start])
         halves.append(sketched(where, pieces, half_cols, dtype))
     traded = shifted(halves[0], "c", 1)
-    partial = halves[1] + traded.astype(jnp.float32)
-    partial = partial.reshape(ny, examples, half_cols)
+    kept, traded = (h.reshape(ny, examples, half_cols) for h in (halves[1], traded))
     turn = x - y + ny
-    features = part_of(partial, lax.rem(turn, ny))
-    sent = [
-        shifted(part_of(partial, lax.rem(turn + k, ny)).astype(jnp.bfloat16), "x", k)
-        for k in range(1, nx)
+    sums = [
+        part_of(kept, lax.rem(turn + k, ny)) + part_of(traded, lax.rem(turn + k, ny)).astype(jnp.float32)
+        for k in range(nx)
     ]
+    features = sums[0]
+    sent = [shifted(sums[k].astype(jnp.bfloat16), "x", k) for k in range(1, nx)]
     for part in sent:
         features = features + part.astype(jnp.float32)
     feature_scale = 1.0 / math.sqrt(L * R * VW)

time: 171 us -> 170 us (level)
  Pallas kernels: 9.18 us -> 6.18 us
    pallas_call x2, Pallas kernels: 9.18 us -> 6.18 us  [sketched(): pl.pallas_call(sketch_kernel, out_shape=jax.ShapeDtypeStruct((rows, cols)...]
  transfers between devices with their start and end apart: 20 -> 20, of which waited for: 10 -> 10; matrix products, arithmetic and copies ran while one was open for 6% -> 6% of each run, Pallas kernels for 3% -> 2%
where the time goes in v4:
time: 170 us; the launch traced here: 168 us
  starting transfers between devices  95.7 us (56%)
  waiting for transfers between devices  46.7 us (27%)
  matrix products  7.36 us (4%)
  local copies, waits for them, and re-layouts  6.59 us (4%)
  Pallas kernels  6.18 us (4%)
  other arithmetic  3.32 us (2%)
  between operations  1.77 us (1%)
    ppermute x14, starting transfers between devices, shifted(): lax.ppermute(value, axes, [(k, (k + shift) % size) for k in range(size)])  48.2 us
    all_to_all x3, starting transfers between devices, swap(): return lax.all_to_all(parts, axes, split_axis=0, concat_axis=0, tiled=True)  38.6 us
    ppermute x14, waiting for transfers between devices, shifted(): lax.ppermute(value, axes, [(k, (k + shift) % size) for k in range(size)])  30.9 us
    all_to_all x3, waiting for transfers between devices, swap(): return lax.all_to_all(parts, axes, split_axis=0, concat_axis=0, tiled=True)  10.6 us
    ppermute x3, starting transfers between devices, shards(): lax.ppermute(scores, axis, [(k, k ^ bit) for k in range(size)])  8.94 us
    pallas_call x2, Pallas kernels, sketched(): pl.pallas_call(sketch_kernel, out_shape=jax.ShapeDtypeStruct((rows, cols)...  6.18 us
    ppermute x3, waiting for transfers between devices, shards(): lax.ppermute(scores, axis, [(k, k ^ bit) for k in range(size)])  5.22 us
    dot_general x2, matrix products, shards(): jnp.einsum('tmk,nk->tmn', cols, part_of(rows, h), preferred_element_type=...  4.15 us
  transfers between devices with their start and end apart: 20, of which 10 were waited for; matrix products, arithmetic and copies ran while one was open for 6% of the time, Pallas kernels for 2%

profile of v4, /device:TPU:1, one launch (start us, length us, event | category | flops | bytes accessed | tf_op | source)
XLA Modules:
  0.0 167.6 jit_solution(14758159525779706732)
XLA Ops:
  3.3 4.0 %collective-permute-start.2 = (bf16[16,64,128]{2,1,0:T(8,128)(2,1)S(1)}, bf16[16,64,128]{2,1,0:T(8,128)(2,1)S(1)}, u32[]{:S(2)}, u32[]{:S(2)}) collective-permute-start(bf16[16,64,128]{2,1,0:T(8,128)(2,1)S(1)} %bitcast.71), channel_id=1, source_target_pairs={{0,128},{128,256},{256,384},{384,0},{1,129},{129,257},{257,385},{3... | collective-permute-start | bytes 786440 | tf_op jit(solution)/shard_map/ppermute | solution.py:34
  7.3 4.5 %collective-permute-start.1 = (bf16[16,64,128]{2,1,0:T(8,128)(2,1)S(1)}, bf16[16,64,128]{2,1,0:T(8,128)(2,1)S(1)}, u32[]{:S(2)}, u32[]{:S(2)}) collective-permute-start(bf16[16,64,128]{2,1,0:T(8,128)(2,1)S(1)} %bitcast.72), channel_id=1, source_target_pairs={{0,256},{128,384},{256,0},{384,128},{1,257},{129,385},{257,1},{385... | collective-permute-start | bytes 786440 | tf_op jit(solution)/shard_map/ppermute | solution.py:34
  11.8 3.0 %collective-permute-start = (bf16[16,64,128]{2,1,0:T(8,128)(2,1)S(1)}, bf16[16,64,128]{2,1,0:T(8,128)(2,1)S(1)}, u32[]{:S(2)}, u32[]{:S(2)}) collective-permute-start(bf16[16,64,128]{2,1,0:T(8,128)(2,1)S(1)} %bitcast.73), channel_id=1, source_target_pairs={{0,384},{128,0},{256,128},{384,256},{1,385},{129,1},{257,129},{385... | collective-permute-start | bytes 786440 | tf_op jit(solution)/shard_map/ppermute | solution.py:34
  15.6 5.0 %collective-permute-done.1.refs_2_ = bf16[16,64,128]{2,1,0:T(8,128)(2,1)S(1)} collective-permute-done((bf16[16,64,128]{2,1,0:T(8,128)(2,1)S(1)}, bf16[16,64,128]{2,1,0:T(8,128)(2,1)S(1)}, u32[]{:S(2)}, u32[]{:S(2)}) %collective-permute-start.1) | collective-permute-done | bytes 262176 | tf_op jit(solution)/shard_map/ppermute | solution.py:34
  20.6 3.1 %sketch.3 = bf16[256,1024]{1,0:T(8,128)(2,1)S(1)} custom-call(s32[3]{0:T(128)S(1)} %pad_add_fusion.2.where, bf16[16,64,128]{2,1,0:T(8,128)(2,1)S(1)} %bitcast.74, bf16[16,64,128]{2,1,0:T(8,128)(2,1)S(1)} %collective-permute-done.refs_1_, bf16[16,64,128]{2,1,0:T(8,128)(2,1)S(1)} %collective-permute-done.1.refs_2_, ...), custom_call_target="tpu_custom_call" | custom-call | flops 1073741824 | bytes 1048576 | tf_op jit(solution)/shard_map/sketch/pallas_call | solution.py:86
  23.7 6.6 %collective-permute-start.3 = (bf16[256,1024]{1,0:T(8,128)(2,1)S(1)}, bf16[256,1024]{1,0:T(8,128)(2,1)}, u32[]{:S(2)}, u32[]{:S(2)}) collective-permute-start(bf16[256,1024]{1,0:T(8,128)(2,1)S(1)} %sketch.3), channel_id=1, source_target_pairs={{0,1},{1,0},{2,3},{3,2},{4,5},{5,4},{6,7},{7,6},{8,9},{9,8},{10,11... | collective-permute-start | bytes 1572872 | tf_op jit(solution)/shard_map/ppermute | solution.py:34
  31.4 3.1 %sketch.2 = f32[256,1024]{1,0:T(8,128)S(1)} custom-call(s32[3]{0:T(128)S(1)} %pad_add_fusion.where, bf16[16,64,128]{2,1,0:T(8,128)(2,1)S(1)} %bitcast.75, bf16[16,64,128]{2,1,0:T(8,128)(2,1)S(1)} %copy-done.2, bf16[16,64,128]{2,1,0:T(8,128)(2,1)S(1)} %collective-permute-done.1.refs_2_, bf16[16,64,128]{2,1,0:T(8,128)(2,1)S(1)} %collective-permute-done.2.refs_3_), custom_call_target="tpu_custom_call" | custom-call | flops 1073741824 | bytes 1048576 | tf_op jit(solution)/shard_map/sketch/pallas_call | solution.py:86
  35.6 1.9 %collective-permute-start.4 = (bf16[64,1024]{1,0:T(8,128)(2,1)S(1)}, bf16[64,1024]{1,0:T(8,128)(2,1)S(1)}, u32[]{:S(2)}, u32[]{:S(2)}) collective-permute-start(bf16[64,1024]{1,0:T(8,128)(2,1)S(1)} %get-tuple-element.4), channel_id=1, source_target_pairs={{0,2},{2,4},{4,6},{6,0},{1,3},{3,5},{5,7},{7,1},{8,10},{10,12},{12... | collective-permute-start | bytes 393224 | tf_op jit(solution)/shard_map/ppermute | solution.py:34
  37.6 4.5 %collective-permute-start.6 = (bf16[64,1024]{1,0:T(8,128)(2,1)S(1)}, bf16[64,1024]{1,0:T(8,128)(2,1)S(1)}, u32[]{:S(2)}, u32[]{:S(2)}) collective-permute-start(bf16[64,1024]{1,0:T(8,128)(2,1)S(1)} %get-tuple-element.5), channel_id=1, source_target_pairs={{0,6},{2,0},{4,2},{6,4},{1,7},{3,1},{5,3},{7,5},{8,14},{10,8},{12,... | collective-permute-start | bytes 393224 | tf_op jit(solution)/shard_map/ppermute | solution.py:34
  42.1 2.3 %collective-permute-start.5 = (bf16[64,1024]{1,0:T(8,128)(2,1)S(1)}, bf16[64,1024]{1,0:T(8,128)(2,1)S(1)}, u32[]{:S(2)}, u32[]{:S(2)}) collective-permute-start(bf16[64,1024]{1,0:T(8,128)(2,1)S(1)} %get-tuple-element.6), channel_id=1, source_target_pairs={{0,4},{2,6},{4,0},{6,2},{1,5},{3,7},{5,1},{7,3},{8,12},{10,14},{12... | collective-permute-start | bytes 393224 | tf_op jit(solution)/shard_map/ppermute | solution.py:34
  44.7 5.3 %collective-permute-done.5 = bf16[64,1024]{1,0:T(8,128)(2,1)S(1)} collective-permute-done((bf16[64,1024]{1,0:T(8,128)(2,1)S(1)}, bf16[64,1024]{1,0:T(8,128)(2,1)S(1)}, u32[]{:S(2)}, u32[]{:S(2)}) %collective-permute-start.5) | collective-permute-done | bytes 131104 | tf_op jit(solution)/shard_map/ppermute | solution.py:34
  51.9 13.6 %all-to-all-start = ((bf16[4,64,1024]{2,1,0:T(8,128)(2,1)}), bf16[4,64,1024]{2,1,0:T(8,128)(2,1)S(1)}, u32[]{:S(2)}, u32[]{:S(2)}) async-start(bf16[4,64,1024]{2,1,0:T(8,128)(2,1)} %broadcast_in_dim.24), calls=%async_computation | async-start | bytes 1048576 | tf_op jit(solution)/shard_map/all_to_all | solution.py:25
  67.1 3.6 %collective-permute-start.7 = (bf16[64,1024]{1,0:T(8,128)(2,1)S(1)}, bf16[64,1024]{1,0:T(8,128)(2,1)S(1)}, u32[]{:S(2)}, u32[]{:S(2)}) collective-permute-start(bf16[64,1024]{1,0:T(8,128)(2,1)S(1)} %get-tuple-element.3), channel_id=1, source_target_pairs={{0,24},{8,0},{16,8},{24,16},{1,25},{9,1},{17,9},{25,17},{2,26},{10... | collective-permute-start | bytes 393224 | tf_op jit(solution)/shard_map/ppermute | solution.py:34
  72.1 1.9 %collective-permute-start.9 = (bf16[64,1024]{1,0:T(8,128)(2,1)S(1)}, bf16[64,1024]{1,0:T(8,128)(2,1)S(1)}, u32[]{:S(2)}, u32[]{:S(2)}) collective-permute-start(bf16[64,1024]{1,0:T(8,128)(2,1)S(1)} %get-tuple-element.3), channel_id=1, source_target_pairs={{0,8},{8,16},{16,24},{24,0},{1,9},{9,17},{17,25},{25,1},{2,10},{10... | collective-permute-start | bytes 393224 | tf_op jit(solution)/shard_map/ppermute | solution.py:34
  74.0 2.9 %collective-permute-start.8 = (bf16[64,1024]{1,0:T(8,128)(2,1)S(1)}, bf16[64,1024]{1,0:T(8,128)(2,1)S(1)}, u32[]{:S(2)}, u32[]{:S(2)}) collective-permute-start(bf16[64,1024]{1,0:T(8,128)(2,1)S(1)} %get-tuple-element.3), channel_id=1, source_target_pairs={{0,16},{8,24},{16,0},{24,8},{1,17},{9,25},{17,1},{25,9},{2,18},{10... | collective-permute-start | bytes 393224 | tf_op jit(solution)/shard_map/ppermute | solution.py:34
  77.0 10.6 %all-to-all-done = bf16[4,64,1024]{2,1,0:T(8,128)(2,1)S(1)} async-done(((bf16[4,64,1024]{2,1,0:T(8,128)(2,1)}), bf16[4,64,1024]{2,1,0:T(8,128)(2,1)S(1)}, u32[]{:S(2)}, u32[]{:S(2)}) %all-to-all-start) | async-done | bytes 524320 | tf_op jit(solution)/shard_map/all_to_all | solution.py:25
  87.5 18.2 %all-to-all-start.2 = ((bf16[64,2,2048]{2,1,0:T(2,128)(2,1)}), bf16[64,2,2048]{2,1,0:T(2,128)(2,1)S(1)}, u32[]{:S(2)}, u32[]{:S(2)}) async-start(bf16[64,2,2048]{2,1,0:T(2,128)(2,1)} %reshape.73), calls=%async_computation.2 | async-start | bytes 1048576 | tf_op jit(solution)/shard_map/all_to_all | solution.py:25
  105.8 1.9 %collective-permute-start.12 = (bf16[256,1024]{1,0:T(8,128)(2,1)S(1)}, bf16[256,1024]{1,0:T(8,128)(2,1)}, u32[]{:S(2)}, u32[]{:S(2)}) collective-permute-start(bf16[256,1024]{1,0:T(8,128)(2,1)S(1)} %bitcast.80), channel_id=1, source_target_pairs={{0,2},{2,4},{4,6},{6,0},{1,3},{3,5},{5,7},{7,1},{8,10},{10,12},{12... | collective-permute-start | bytes 1572872 | tf_op jit(solution)/shard_map/ppermute | solution.py:34
  107.8 4.3 %collective-permute-start.11 = (bf16[256,1024]{1,0:T(8,128)(2,1)S(1)}, bf16[256,1024]{1,0:T(8,128)(2,1)}, u32[]{:S(2)}, u32[]{:S(2)}) collective-permute-start(bf16[256,1024]{1,0:T(8,128)(2,1)S(1)} %bitcast.81), channel_id=1, source_target_pairs={{0,4},{2,6},{4,0},{6,2},{1,5},{3,7},{5,1},{7,3},{8,12},{10,14},{12... | collective-permute-start | bytes 1572872 | tf_op jit(solution)/shard_map/ppermute | solution.py:34
  112.1 3.1 %collective-permute-start.10 = (bf16[256,1024]{1,0:T(8,128)(2,1)S(1)}, bf16[256,1024]{1,0:T(8,128)(2,1)}, u32[]{:S(2)}, u32[]{:S(2)}) collective-permute-start(bf16[256,1024]{1,0:T(8,128)(2,1)S(1)} %bitcast.82), channel_id=1, source_target_pairs={{0,6},{2,0},{4,2},{6,4},{1,7},{3,1},{5,3},{7,5},{8,14},{10,8},{12,... | collective-permute-start | bytes 1572872 | tf_op jit(solution)/shard_map/ppermute | solution.py:34
  115.2 5.5 %collective-permute-done.12 = bf16[256,1024]{1,0:T(8,128)(2,1)} collective-permute-done((bf16[256,1024]{1,0:T(8,128)(2,1)S(1)}, bf16[256,1024]{1,0:T(8,128)(2,1)}, u32[]{:S(2)}, u32[]{:S(2)}) %collective-permute-start.12) | collective-permute-done | bytes 524320 | tf_op jit(solution)/shard_map/ppermute | solution.py:34
  120.7 10.9 %collective-permute-done.11 = bf16[256,1024]{1,0:T(8,128)(2,1)} collective-permute-done((bf16[256,1024]{1,0:T(8,128)(2,1)S(1)}, bf16[256,1024]{1,0:T(8,128)(2,1)}, u32[]{:S(2)}, u32[]{:S(2)}) %collective-permute-start.11) | collective-permute-done | bytes 524320 | tf_op jit(solution)/shard_map/ppermute | solution.py:34
  131.5 4.0 %collective-permute-done.10 = bf16[256,1024]{1,0:T(8,128)(2,1)} collective-permute-done((bf16[256,1024]{1,0:T(8,128)(2,1)S(1)}, bf16[256,1024]{1,0:T(8,128)(2,1)}, u32[]{:S(2)}, u32[]{:S(2)}) %collective-permute-start.10) | collective-permute-done | bytes 524320 | tf_op jit(solution)/shard_map/ppermute | solution.py:34
  135.5 2.1 %convolution_convert_fusion.2 = bf16[4,256,128]{2,1,0:T(8,128)(2,1)S(1)} fusion(bf16[1,256,1024]{2,1,0:T(8,128)(2,1)} %bitcast.18, bf16[1,256,1024]{2,1,0:T(8,128)(2,1)} %bitcast.17, bf16[1,256,1024]{2,1,0:T(8,128)(2,1)} %bitcast.16, bf16[1,256,1024]{2,1,0:T(8,128)(2,1)S(1)} %bitcast.83, bf16[2,128,1024]{2,1,0:T(8,128)(2,1)S(1)} %bitcast.85, s32[]{:T(128)S(6)} %select_n.59), kind=kOutput, calls=%fused_computation.3 | convolution fusion | flops 271712256 | bytes 2621444 | tf_op jit(solution)/shard_map/tmk,nk->tmn/dot_general | solution.py:163
  137.6 3.6 %collective-permute-start.13 = (bf16[4,256,128]{2,1,0:T(8,128)(2,1)S(1)}, bf16[4,256,128]{2,1,0:T(8,128)(2,1)S(1)}, u32[]{:S(2)}, u32[]{:S(2)}) collective-permute-start(bf16[4,256,128]{2,1,0:T(8,128)(2,1)S(1)} %convolution_convert_fusion.2), channel_id=1, source_target_pairs={{0,1},{1,0},{2,3},{3,2},{4,5},{5,4},{6,7},{7,6},{8,9},{9,8},{10,11... | collective-permute-start | bytes 786440 | tf_op jit(solution)/shard_map/ppermute | solution.py:34
  141.2 2.1 %fusion = f32[4,256,128]{2,1,0:T(8,128)S(1)} fusion(bf16[1,256,1024]{2,1,0:T(8,128)(2,1)} %bitcast.18, bf16[1,256,1024]{2,1,0:T(8,128)(2,1)} %bitcast.17, bf16[1,256,1024]{2,1,0:T(8,128)(2,1)} %bitcast.16, bf16[1,256,1024]{2,1,0:T(8,128)(2,1)S(1)} %bitcast.84, bf16[2,128,1024]{2,1,0:T(8,128)(2,1)S(1)} %bitcast.86, s32[]{:T(128)S(6)} %select_n.58), kind=kOutput, calls=%fused_computation.7 | convolution fusion | flops 271581184 | bytes 2883588 | tf_op jit(solution)/shard_map/tmk,nk->tmn/dot_general | solution.py:163
  144.1 6.7 %all-to-all-start.1 = ((bf16[16,64,128]{2,1,0:T(8,128)(2,1)}), bf16[16,64,128]{2,1,0:T(8,128)(2,1)S(1)}, u32[]{:S(2)}, u32[]{:S(2)}) async-start(bf16[16,64,128]{2,1,0:T(8,128)(2,1)} %bitcast.24), calls=%async_computation.1 | async-start | bytes 524288 | tf_op jit(solution)/shard_map/all_to_all | solution.py:25
  151.4 2.2 %collective-permute-start.14 = (f32[64,128]{1,0:T(8,128)S(1)}, f32[64,128]{1,0:T(8,128)S(1)}, u32[]{:S(2)}, u32[]{:S(2)}) collective-permute-start(f32[64,128]{1,0:T(8,128)S(1)} %reshape.76), channel_id=1, source_target_pairs={{0,1},{1,0},{2,3},{3,2},{4,5},{5,4},{6,7},{7,6},{8,9},{9,8},{10,11... | collective-permute-start | bytes 98312 | tf_op jit(solution)/shard_map/ppermute | solution.py:185
  154.5 2.8 %collective-permute-start.15 = (f32[64,128]{1,0:T(8,128)S(1)}, f32[64,128]{1,0:T(8,128)S(1)}, u32[]{:S(2)}, u32[]{:S(2)}) collective-permute-start(f32[64,128]{1,0:T(8,128)S(1)} %add.190), channel_id=1, source_target_pairs={{0,2},{2,0},{4,6},{6,4},{1,3},{3,1},{5,7},{7,5},{8,10},{10,8},{12,... | collective-permute-start | bytes 98312 | tf_op jit(solution)/shard_map/ppermute | solution.py:185
  157.3 2.2 %collective-permute-done.15 = f32[64,128]{1,0:T(8,128)S(1)} collective-permute-done((f32[64,128]{1,0:T(8,128)S(1)}, f32[64,128]{1,0:T(8,128)S(1)}, u32[]{:S(2)}, u32[]{:S(2)}) %collective-permute-start.15) | collective-permute-done | bytes 32800 | tf_op jit(solution)/shard_map/ppermute | solution.py:185
  159.4 4.0 %collective-permute-start.16 = (f32[64,128]{1,0:T(8,128)S(1)}, f32[64,128]{1,0:T(8,128)S(1)}, u32[]{:S(2)}, u32[]{:S(2)}) collective-permute-start(f32[64,128]{1,0:T(8,128)S(1)} %add.191), channel_id=1, source_target_pairs={{0,4},{2,6},{4,0},{6,2},{1,5},{3,7},{5,1},{7,3},{8,12},{10,14},{12... | collective-permute-start | bytes 98312 | tf_op jit(solution)/shard_map/ppermute | solution.py:185
  163.4 2.2 %collective-permute-done.16 = f32[64,128]{1,0:T(8,128)S(1)} collective-permute-done((f32[64,128]{1,0:T(8,128)S(1)}, f32[64,128]{1,0:T(8,128)S(1)}, u32[]{:S(2)}, u32[]{:S(2)}) %collective-permute-start.16) | collective-permute-done | bytes 32800 | tf_op jit(solution)/shard_map/ppermute | solution.py:185
  (53 shorter events, 14.3 us)
Async XLA Ops:
  0.6 1.2 copy-start
  3.3 12.3 %collective-permute-start.2 = (bf16[16,64,128]{2,1,0:T(8,128)(2,1)S(1)}, bf16[16,64,128]{2,1,0:T(8,128)(2,1)S(1)}, u32[]{:S(2)}, u32[]{:S(2)}) collective-permute-start(bf16[16,64,128]{2,1,0:T(8,128)(2,1)S(1)} %bitcast.71), channel_id=1, source_target_pairs={{0,128},{128,256},{256,384},{384,0},{1,129},{129,257},{257,385},{3... | collective-permute-start | bytes 786440 | tf_op jit(solution)/shard_map/ppermute | solution.py:34
  7.3 13.3 %collective-permute-start.1 = (bf16[16,64,128]{2,1,0:T(8,128)(2,1)S(1)}, bf16[16,64,128]{2,1,0:T(8,128)(2,1)S(1)}, u32[]{:S(2)}, u32[]{:S(2)}) collective-permute-start(bf16[16,64,128]{2,1,0:T(8,128)(2,1)S(1)} %bitcast.72), channel_id=1, source_target_pairs={{0,256},{128,384},{256,0},{384,128},{1,257},{129,385},{257,1},{385... | collective-permute-start | bytes 786440 | tf_op jit(solution)/shard_map/ppermute | solution.py:34
  11.8 8.7 %collective-permute-start = (bf16[16,64,128]{2,1,0:T(8,128)(2,1)S(1)}, bf16[16,64,128]{2,1,0:T(8,128)(2,1)S(1)}, u32[]{:S(2)}, u32[]{:S(2)}) collective-permute-start(bf16[16,64,128]{2,1,0:T(8,128)(2,1)S(1)} %bitcast.73), channel_id=1, source_target_pairs={{0,384},{128,0},{256,128},{384,256},{1,385},{129,1},{257,129},{385... | collective-permute-start | bytes 786440 | tf_op jit(solution)/shard_map/ppermute | solution.py:34
  20.6 3.1 %copy-start.1 = (bf16[16,64,128]{2,1,0:T(8,128)(2,1)}, bf16[16,64,128]{2,1,0:T(8,128)(2,1)S(1)}, u32[]{:S(2)}) copy-start(bf16[16,64,128]{2,1,0:T(8,128)(2,1)S(1)} %collective-permute-done.refs_1_) | copy-start | bytes 786436
  23.7 10.8 %collective-permute-start.3 = (bf16[256,1024]{1,0:T(8,128)(2,1)S(1)}, bf16[256,1024]{1,0:T(8,128)(2,1)}, u32[]{:S(2)}, u32[]{:S(2)}) collective-permute-start(bf16[256,1024]{1,0:T(8,128)(2,1)S(1)} %sketch.3), channel_id=1, source_target_pairs={{0,1},{1,0},{2,3},{3,2},{4,5},{5,4},{6,7},{7,6},{8,9},{9,8},{10,11... | collective-permute-start | bytes 1572872 | tf_op jit(solution)/shard_map/ppermute | solution.py:34
  30.4 1.0 copy-start.2
  35.6 8.8 %collective-permute-start.4 = (bf16[64,1024]{1,0:T(8,128)(2,1)S(1)}, bf16[64,1024]{1,0:T(8,128)(2,1)S(1)}, u32[]{:S(2)}, u32[]{:S(2)}) collective-permute-start(bf16[64,1024]{1,0:T(8,128)(2,1)S(1)} %get-tuple-element.4), channel_id=1, source_target_pairs={{0,2},{2,4},{4,6},{6,0},{1,3},{3,5},{5,7},{7,1},{8,10},{10,12},{12... | collective-permute-start | bytes 393224 | tf_op jit(solution)/shard_map/ppermute | solution.py:34
  37.6 7.1 %collective-permute-start.6 = (bf16[64,1024]{1,0:T(8,128)(2,1)S(1)}, bf16[64,1024]{1,0:T(8,128)(2,1)S(1)}, u32[]{:S(2)}, u32[]{:S(2)}) collective-permute-start(bf16[64,1024]{1,0:T(8,128)(2,1)S(1)} %get-tuple-element.5), channel_id=1, source_target_pairs={{0,6},{2,0},{4,2},{6,4},{1,7},{3,1},{5,3},{7,5},{8,14},{10,8},{12,... | collective-permute-start | bytes 393224 | tf_op jit(solution)/shard_map/ppermute | solution.py:34
  42.1 7.9 %collective-permute-start.5 = (bf16[64,1024]{1,0:T(8,128)(2,1)S(1)}, bf16[64,1024]{1,0:T(8,128)(2,1)S(1)}, u32[]{:S(2)}, u32[]{:S(2)}) collective-permute-start(bf16[64,1024]{1,0:T(8,128)(2,1)S(1)} %get-tuple-element.6), channel_id=1, source_target_pairs={{0,4},{2,6},{4,0},{6,2},{1,5},{3,7},{5,1},{7,3},{8,12},{10,14},{12... | collective-permute-start | bytes 393224 | tf_op jit(solution)/shard_map/ppermute | solution.py:34
  51.1 14.5 %copy-start.4 = (s32[64,1]{0,1:T(1,128)S(1)}, s32[64,1]{0,1:T(1,128)}, u32[]{:S(2)}) copy-start(s32[64,1]{0,1:T(1,128)} %param.10) | copy-start | bytes 772
  51.1 14.7 %copy-start.3 = (bf16[64,64,128]{2,1,0:T(8,128)(2,1)S(1)}, bf16[64,64,128]{2,1,0:T(8,128)(2,1)}, u32[]{:S(2)}) copy-start(bf16[64,64,128]{2,1,0:T(8,128)(2,1)} %param.9) | copy-start | bytes 3145732
  51.9 35.6 %all-to-all-start = ((bf16[4,64,1024]{2,1,0:T(8,128)(2,1)}), bf16[4,64,1024]{2,1,0:T(8,128)(2,1)S(1)}, u32[]{:S(2)}, u32[]{:S(2)}) async-start(bf16[4,64,1024]{2,1,0:T(8,128)(2,1)} %broadcast_in_dim.24), calls=%async_computation | async-start | bytes 1048576 | tf_op jit(solution)/shard_map/all_to_all | solution.py:25
  67.1 38.6 %collective-permute-start.7 = (bf16[64,1024]{1,0:T(8,128)(2,1)S(1)}, bf16[64,1024]{1,0:T(8,128)(2,1)S(1)}, u32[]{:S(2)}, u32[]{:S(2)}) collective-permute-start(bf16[64,1024]{1,0:T(8,128)(2,1)S(1)} %get-tuple-element.3), channel_id=1, source_target_pairs={{0,24},{8,0},{16,8},{24,16},{1,25},{9,1},{17,9},{25,17},{2,26},{10... | collective-permute-start | bytes 393224 | tf_op jit(solution)/shard_map/ppermute | solution.py:34
  72.1 33.7 %collective-permute-start.9 = (bf16[64,1024]{1,0:T(8,128)(2,1)S(1)}, bf16[64,1024]{1,0:T(8,128)(2,1)S(1)}, u32[]{:S(2)}, u32[]{:S(2)}) collective-permute-start(bf16[64,1024]{1,0:T(8,128)(2,1)S(1)} %get-tuple-element.3), channel_id=1, source_target_pairs={{0,8},{8,16},{16,24},{24,0},{1,9},{9,17},{17,25},{25,1},{2,10},{10... | collective-permute-start | bytes 393224 | tf_op jit(solution)/shard_map/ppermute | solution.py:34
  74.0 31.7 %collective-permute-start.8 = (bf16[64,1024]{1,0:T(8,128)(2,1)S(1)}, bf16[64,1024]{1,0:T(8,128)(2,1)S(1)}, u32[]{:S(2)}, u32[]{:S(2)}) collective-permute-start(bf16[64,1024]{1,0:T(8,128)(2,1)S(1)} %get-tuple-element.3), channel_id=1, source_target_pairs={{0,16},{8,24},{16,0},{24,8},{1,17},{9,25},{17,1},{25,9},{2,18},{10... | collective-permute-start | bytes 393224 | tf_op jit(solution)/shard_map/ppermute | solution.py:34
  87.5 56.6 %all-to-all-start.2 = ((bf16[64,2,2048]{2,1,0:T(2,128)(2,1)}), bf16[64,2,2048]{2,1,0:T(2,128)(2,1)S(1)}, u32[]{:S(2)}, u32[]{:S(2)}) async-start(bf16[64,2,2048]{2,1,0:T(2,128)(2,1)} %reshape.73), calls=%async_computation.2 | async-start | bytes 1048576 | tf_op jit(solution)/shard_map/all_to_all | solution.py:25
  105.8 14.8 %collective-permute-start.12 = (bf16[256,1024]{1,0:T(8,128)(2,1)S(1)}, bf16[256,1024]{1,0:T(8,128)(2,1)}, u32[]{:S(2)}, u32[]{:S(2)}) collective-permute-start(bf16[256,1024]{1,0:T(8,128)(2,1)S(1)} %bitcast.80), channel_id=1, source_target_pairs={{0,2},{2,4},{4,6},{6,0},{1,3},{3,5},{5,7},{7,1},{8,10},{10,12},{12... | collective-permute-start | bytes 1572872 | tf_op jit(solution)/shard_map/ppermute | solution.py:34
  107.8 23.7 %collective-permute-start.11 = (bf16[256,1024]{1,0:T(8,128)(2,1)S(1)}, bf16[256,1024]{1,0:T(8,128)(2,1)}, u32[]{:S(2)}, u32[]{:S(2)}) collective-permute-start(bf16[256,1024]{1,0:T(8,128)(2,1)S(1)} %bitcast.81), channel_id=1, source_target_pairs={{0,4},{2,6},{4,0},{6,2},{1,5},{3,7},{5,1},{7,3},{8,12},{10,14},{12... | collective-permute-start | bytes 1572872 | tf_op jit(solution)/shard_map/ppermute | solution.py:34
  112.1 23.4 %collective-permute-start.10 = (bf16[256,1024]{1,0:T(8,128)(2,1)S(1)}, bf16[256,1024]{1,0:T(8,128)(2,1)}, u32[]{:S(2)}, u32[]{:S(2)}) collective-permute-start(bf16[256,1024]{1,0:T(8,128)(2,1)S(1)} %bitcast.82), channel_id=1, source_target_pairs={{0,6},{2,0},{4,2},{6,4},{1,7},{3,1},{5,3},{7,5},{8,14},{10,8},{12,... | collective-permute-start | bytes 1572872 | tf_op jit(solution)/shard_map/ppermute | solution.py:34
  137.6 5.7 %collective-permute-start.13 = (bf16[4,256,128]{2,1,0:T(8,128)(2,1)S(1)}, bf16[4,256,128]{2,1,0:T(8,128)(2,1)S(1)}, u32[]{:S(2)}, u32[]{:S(2)}) collective-permute-start(bf16[4,256,128]{2,1,0:T(8,128)(2,1)S(1)} %convolution_convert_fusion.2), channel_id=1, source_target_pairs={{0,1},{1,0},{2,3},{3,2},{4,5},{5,4},{6,7},{7,6},{8,9},{9,8},{10,11... | collective-permute-start | bytes 786440 | tf_op jit(solution)/shard_map/ppermute | solution.py:34
  144.1 22.2 %all-to-all-start.1 = ((bf16[16,64,128]{2,1,0:T(8,128)(2,1)}), bf16[16,64,128]{2,1,0:T(8,128)(2,1)S(1)}, u32[]{:S(2)}, u32[]{:S(2)}) async-start(bf16[16,64,128]{2,1,0:T(8,128)(2,1)} %bitcast.24), calls=%async_computation.1 | async-start | bytes 524288 | tf_op jit(solution)/shard_map/all_to_all | solution.py:25
  151.4 3.1 %collective-permute-start.14 = (f32[64,128]{1,0:T(8,128)S(1)}, f32[64,128]{1,0:T(8,128)S(1)}, u32[]{:S(2)}, u32[]{:S(2)}) collective-permute-start(f32[64,128]{1,0:T(8,128)S(1)} %reshape.76), channel_id=1, source_target_pairs={{0,1},{1,0},{2,3},{3,2},{4,5},{5,4},{6,7},{7,6},{8,9},{9,8},{10,11... | collective-permute-start | bytes 98312 | tf_op jit(solution)/shard_map/ppermute | solution.py:185
  154.5 4.9 %collective-permute-start.15 = (f32[64,128]{1,0:T(8,128)S(1)}, f32[64,128]{1,0:T(8,128)S(1)}, u32[]{:S(2)}, u32[]{:S(2)}) collective-permute-start(f32[64,128]{1,0:T(8,128)S(1)} %add.190), channel_id=1, source_target_pairs={{0,2},{2,0},{4,6},{6,4},{1,3},{3,1},{5,7},{7,5},{8,10},{10,8},{12,... | collective-permute-start | bytes 98312 | tf_op jit(solution)/shard_map/ppermute | solution.py:185
  159.4 6.2 %collective-permute-start.16 = (f32[64,128]{1,0:T(8,128)S(1)}, f32[64,128]{1,0:T(8,128)S(1)}, u32[]{:S(2)}, u32[]{:S(2)}) collective-permute-start(f32[64,128]{1,0:T(8,128)S(1)} %add.191), channel_id=1, source_target_pairs={{0,4},{2,6},{4,0},{6,2},{1,5},{3,7},{5,1},{7,3},{8,12},{10,14},{12... | collective-permute-start | bytes 98312 | tf_op jit(solution)/shard_map/ppermute | solution.py:185

commit v5 on v4

--- a/solution.py
+++ b/solution.py
@@ -148,7 +148,9 @@
         for k in range(nx)
     ]
     features = sums[0]
-    sent = [shifted(sums[k].astype(jnp.bfloat16), "x", k) for k in range(1, nx)]
+    sent = []
+    for k in range(1, nx):
+        sent.append(shifted(sums[k].astype(jnp.bfloat16), "x", k))
     for part in sent:
         features = features + part.astype(jnp.float32)
     feature_scale = 1.0 / math.sqrt(L * R * VW)
@@ -158,7 +160,10 @@
     near = placed_at(near, [lax.rem(zl + k, nzl) for k in range(nzl)])
     near = near.reshape(nzl * examples, -1)
     rows = from_everyone(features, "zh").reshape(nc, (nzh // nc) * examples, -1)
-    cols = jnp.stack([near] + [shifted(near, "x", -k) for k in range(1, nx)])
+    cols = [near]
+    for k in range(1, nx):
+        cols.append(shifted(near, "x", -k))
+    cols = jnp.stack(cols)
     kept, given = (
         jnp.einsum("tmk,nk->tmn", cols, part_of(rows, h), preferred_element_type=jnp.float32)
         for h in (c, 1 - c)

time: 170 us -> 170 us (level)
  no operation moved by 1% of the time
where the time goes in v5:
time: 170 us; the launch traced here: 168 us
  starting transfers between devices  95.7 us (56%)
  waiting for transfers between devices  46.7 us (27%)
  matrix products  7.36 us (4%)
  local copies, waits for them, and re-layouts  6.59 us (4%)
  Pallas kernels  6.18 us (4%)
  other arithmetic  3.32 us (2%)
  between operations  1.77 us (1%)
    ppermute x14, starting transfers between devices, shifted(): lax.ppermute(value, axes, [(k, (k + shift) % size) for k in range(size)])  48.2 us
    all_to_all x3, starting transfers between devices, swap(): return lax.all_to_all(parts, axes, split_axis=0, concat_axis=0, tiled=True)  38.6 us
    ppermute x14, waiting for transfers between devices, shifted(): lax.ppermute(value, axes, [(k, (k + shift) % size) for k in range(size)])  30.9 us
    all_to_all x3, waiting for transfers between devices, swap(): return lax.all_to_all(parts, axes, split_axis=0, concat_axis=0, tiled=True)  10.6 us
    ppermute x3, starting transfers between devices, shards(): lax.ppermute(scores, axis, [(k, k ^ bit) for k in range(size)])  8.94 us
    pallas_call x2, Pallas kernels, sketched(): pl.pallas_call(sketch_kernel, out_shape=jax.ShapeDtypeStruct((rows, cols)...  6.18 us
    ppermute x3, waiting for transfers between devices, shards(): lax.ppermute(scores, axis, [(k, k ^ bit) for k in range(size)])  5.22 us
    dot_general x2, matrix products, shards(): jnp.einsum('tmk,nk->tmn', cols, part_of(rows, h), preferred_element_type=...  4.15 us
  transfers between devices with their start and end apart: 20, of which 10 were waited for; matrix products, arithmetic and copies ran while one was open for 6% of the time, Pallas kernels for 2%

profile of v5, /device:TPU:1, one launch (start us, length us, event | category | flops | bytes accessed | tf_op | source)
XLA Modules:
  0.0 167.6 jit_solution(14758159525779706732)
XLA Ops:
  3.3 4.0 %collective-permute-start.2 = (bf16[16,64,128]{2,1,0:T(8,128)(2,1)S(1)}, bf16[16,64,128]{2,1,0:T(8,128)(2,1)S(1)}, u32[]{:S(2)}, u32[]{:S(2)}) collective-permute-start(bf16[16,64,128]{2,1,0:T(8,128)(2,1)S(1)} %bitcast.71), channel_id=1, source_target_pairs={{0,128},{128,256},{256,384},{384,0},{1,129},{129,257},{257,385},{3... | collective-permute-start | bytes 786440 | tf_op jit(solution)/shard_map/ppermute | solution.py:34
  7.3 4.5 %collective-permute-start.1 = (bf16[16,64,128]{2,1,0:T(8,128)(2,1)S(1)}, bf16[16,64,128]{2,1,0:T(8,128)(2,1)S(1)}, u32[]{:S(2)}, u32[]{:S(2)}) collective-permute-start(bf16[16,64,128]{2,1,0:T(8,128)(2,1)S(1)} %bitcast.72), channel_id=1, source_target_pairs={{0,256},{128,384},{256,0},{384,128},{1,257},{129,385},{257,1},{385... | collective-permute-start | bytes 786440 | tf_op jit(solution)/shard_map/ppermute | solution.py:34
  11.8 3.0 %collective-permute-start = (bf16[16,64,128]{2,1,0:T(8,128)(2,1)S(1)}, bf16[16,64,128]{2,1,0:T(8,128)(2,1)S(1)}, u32[]{:S(2)}, u32[]{:S(2)}) collective-permute-start(bf16[16,64,128]{2,1,0:T(8,128)(2,1)S(1)} %bitcast.73), channel_id=1, source_target_pairs={{0,384},{128,0},{256,128},{384,256},{1,385},{129,1},{257,129},{385... | collective-permute-start | bytes 786440 | tf_op jit(solution)/shard_map/ppermute | solution.py:34
  15.6 5.0 %collective-permute-done.1.refs_2_ = bf16[16,64,128]{2,1,0:T(8,128)(2,1)S(1)} collective-permute-done((bf16[16,64,128]{2,1,0:T(8,128)(2,1)S(1)}, bf16[16,64,128]{2,1,0:T(8,128)(2,1)S(1)}, u32[]{:S(2)}, u32[]{:S(2)}) %collective-permute-start.1) | collective-permute-done | bytes 262176 | tf_op jit(solution)/shard_map/ppermute | solution.py:34
  20.6 3.1 %sketch.3 = bf16[256,1024]{1,0:T(8,128)(2,1)S(1)} custom-call(s32[3]{0:T(128)S(1)} %pad_add_fusion.2.where, bf16[16,64,128]{2,1,0:T(8,128)(2,1)S(1)} %bitcast.74, bf16[16,64,128]{2,1,0:T(8,128)(2,1)S(1)} %collective-permute-done.refs_1_, bf16[16,64,128]{2,1,0:T(8,128)(2,1)S(1)} %collective-permute-done.1.refs_2_, ...), custom_call_target="tpu_custom_call" | custom-call | flops 1073741824 | bytes 1048576 | tf_op jit(solution)/shard_map/sketch/pallas_call | solution.py:86
  23.7 6.6 %collective-permute-start.3 = (bf16[256,1024]{1,0:T(8,128)(2,1)S(1)}, bf16[256,1024]{1,0:T(8,128)(2,1)}, u32[]{:S(2)}, u32[]{:S(2)}) collective-permute-start(bf16[256,1024]{1,0:T(8,128)(2,1)S(1)} %sketch.3), channel_id=1, source_target_pairs={{0,1},{1,0},{2,3},{3,2},{4,5},{5,4},{6,7},{7,6},{8,9},{9,8},{10,11... | collective-permute-start | bytes 1572872 | tf_op jit(solution)/shard_map/ppermute | solution.py:34
  31.4 3.1 %sketch.2 = f32[256,1024]{1,0:T(8,128)S(1)} custom-call(s32[3]{0:T(128)S(1)} %pad_add_fusion.where, bf16[16,64,128]{2,1,0:T(8,128)(2,1)S(1)} %bitcast.75, bf16[16,64,128]{2,1,0:T(8,128)(2,1)S(1)} %copy-done.2, bf16[16,64,128]{2,1,0:T(8,128)(2,1)S(1)} %collective-permute-done.1.refs_2_, bf16[16,64,128]{2,1,0:T(8,128)(2,1)S(1)} %collective-permute-done.2.refs_3_), custom_call_target="tpu_custom_call" | custom-call | flops 1073741824 | bytes 1048576 | tf_op jit(solution)/shard_map/sketch/pallas_call | solution.py:86
  35.6 1.9 %collective-permute-start.4 = (bf16[64,1024]{1,0:T(8,128)(2,1)S(1)}, bf16[64,1024]{1,0:T(8,128)(2,1)S(1)}, u32[]{:S(2)}, u32[]{:S(2)}) collective-permute-start(bf16[64,1024]{1,0:T(8,128)(2,1)S(1)} %get-tuple-element.4), channel_id=1, source_target_pairs={{0,2},{2,4},{4,6},{6,0},{1,3},{3,5},{5,7},{7,1},{8,10},{10,12},{12... | collective-permute-start | bytes 393224 | tf_op jit(solution)/shard_map/ppermute | solution.py:34
  37.6 4.5 %collective-permute-start.6 = (bf16[64,1024]{1,0:T(8,128)(2,1)S(1)}, bf16[64,1024]{1,0:T(8,128)(2,1)S(1)}, u32[]{:S(2)}, u32[]{:S(2)}) collective-permute-start(bf16[64,1024]{1,0:T(8,128)(2,1)S(1)} %get-tuple-element.5), channel_id=1, source_target_pairs={{0,6},{2,0},{4,2},{6,4},{1,7},{3,1},{5,3},{7,5},{8,14},{10,8},{12,... | collective-permute-start | bytes 393224 | tf_op jit(solution)/shard_map/ppermute | solution.py:34
  42.1 2.3 %collective-permute-start.5 = (bf16[64,1024]{1,0:T(8,128)(2,1)S(1)}, bf16[64,1024]{1,0:T(8,128)(2,1)S(1)}, u32[]{:S(2)}, u32[]{:S(2)}) collective-permute-start(bf16[64,1024]{1,0:T(8,128)(2,1)S(1)} %get-tuple-element.6), channel_id=1, source_target_pairs={{0,4},{2,6},{4,0},{6,2},{1,5},{3,7},{5,1},{7,3},{8,12},{10,14},{12... | collective-permute-start | bytes 393224 | tf_op jit(solution)/shard_map/ppermute | solution.py:34
  44.7 5.3 %collective-permute-done.5 = bf16[64,1024]{1,0:T(8,128)(2,1)S(1)} collective-permute-done((bf16[64,1024]{1,0:T(8,128)(2,1)S(1)}, bf16[64,1024]{1,0:T(8,128)(2,1)S(1)}, u32[]{:S(2)}, u32[]{:S(2)}) %collective-permute-start.5) | collective-permute-done | bytes 131104 | tf_op jit(solution)/shard_map/ppermute | solution.py:34
  51.9 13.6 %all-to-all-start = ((bf16[4,64,1024]{2,1,0:T(8,128)(2,1)}), bf16[4,64,1024]{2,1,0:T(8,128)(2,1)S(1)}, u32[]{:S(2)}, u32[]{:S(2)}) async-start(bf16[4,64,1024]{2,1,0:T(8,128)(2,1)} %broadcast_in_dim.24), calls=%async_computation | async-start | bytes 1048576 | tf_op jit(solution)/shard_map/all_to_all | solution.py:25
  67.1 3.6 %collective-permute-start.7 = (bf16[64,1024]{1,0:T(8,128)(2,1)S(1)}, bf16[64,1024]{1,0:T(8,128)(2,1)S(1)}, u32[]{:S(2)}, u32[]{:S(2)}) collective-permute-start(bf16[64,1024]{1,0:T(8,128)(2,1)S(1)} %get-tuple-element.3), channel_id=1, source_target_pairs={{0,24},{8,0},{16,8},{24,16},{1,25},{9,1},{17,9},{25,17},{2,26},{10... | collective-permute-start | bytes 393224 | tf_op jit(solution)/shard_map/ppermute | solution.py:34
  72.1 1.9 %collective-permute-start.9 = (bf16[64,1024]{1,0:T(8,128)(2,1)S(1)}, bf16[64,1024]{1,0:T(8,128)(2,1)S(1)}, u32[]{:S(2)}, u32[]{:S(2)}) collective-permute-start(bf16[64,1024]{1,0:T(8,128)(2,1)S(1)} %get-tuple-element.3), channel_id=1, source_target_pairs={{0,8},{8,16},{16,24},{24,0},{1,9},{9,17},{17,25},{25,1},{2,10},{10... | collective-permute-start | bytes 393224 | tf_op jit(solution)/shard_map/ppermute | solution.py:34
  74.0 2.9 %collective-permute-start.8 = (bf16[64,1024]{1,0:T(8,128)(2,1)S(1)}, bf16[64,1024]{1,0:T(8,128)(2,1)S(1)}, u32[]{:S(2)}, u32[]{:S(2)}) collective-permute-start(bf16[64,1024]{1,0:T(8,128)(2,1)S(1)} %get-tuple-element.3), channel_id=1, source_target_pairs={{0,16},{8,24},{16,0},{24,8},{1,17},{9,25},{17,1},{25,9},{2,18},{10... | collective-permute-start | bytes 393224 | tf_op jit(solution)/shard_map/ppermute | solution.py:34
  77.0 10.6 %all-to-all-done = bf16[4,64,1024]{2,1,0:T(8,128)(2,1)S(1)} async-done(((bf16[4,64,1024]{2,1,0:T(8,128)(2,1)}), bf16[4,64,1024]{2,1,0:T(8,128)(2,1)S(1)}, u32[]{:S(2)}, u32[]{:S(2)}) %all-to-all-start) | async-done | bytes 524320 | tf_op jit(solution)/shard_map/all_to_all | solution.py:25
  87.5 18.2 %all-to-all-start.2 = ((bf16[64,2,2048]{2,1,0:T(2,128)(2,1)}), bf16[64,2,2048]{2,1,0:T(2,128)(2,1)S(1)}, u32[]{:S(2)}, u32[]{:S(2)}) async-start(bf16[64,2,2048]{2,1,0:T(2,128)(2,1)} %reshape.73), calls=%async_computation.2 | async-start | bytes 1048576 | tf_op jit(solution)/shard_map/all_to_all | solution.py:25
  105.8 1.9 %collective-permute-start.12 = (bf16[256,1024]{1,0:T(8,128)(2,1)S(1)}, bf16[256,1024]{1,0:T(8,128)(2,1)}, u32[]{:S(2)}, u32[]{:S(2)}) collective-permute-start(bf16[256,1024]{1,0:T(8,128)(2,1)S(1)} %bitcast.80), channel_id=1, source_target_pairs={{0,2},{2,4},{4,6},{6,0},{1,3},{3,5},{5,7},{7,1},{8,10},{10,12},{12... | collective-permute-start | bytes 1572872 | tf_op jit(solution)/shard_map/ppermute | solution.py:34
  107.8 4.3 %collective-permute-start.11 = (bf16[256,1024]{1,0:T(8,128)(2,1)S(1)}, bf16[256,1024]{1,0:T(8,128)(2,1)}, u32[]{:S(2)}, u32[]{:S(2)}) collective-permute-start(bf16[256,1024]{1,0:T(8,128)(2,1)S(1)} %bitcast.81), channel_id=1, source_target_pairs={{0,4},{2,6},{4,0},{6,2},{1,5},{3,7},{5,1},{7,3},{8,12},{10,14},{12... | collective-permute-start | bytes 1572872 | tf_op jit(solution)/shard_map/ppermute | solution.py:34
  112.1 3.1 %collective-permute-start.10 = (bf16[256,1024]{1,0:T(8,128)(2,1)S(1)}, bf16[256,1024]{1,0:T(8,128)(2,1)}, u32[]{:S(2)}, u32[]{:S(2)}) collective-permute-start(bf16[256,1024]{1,0:T(8,128)(2,1)S(1)} %bitcast.82), channel_id=1, source_target_pairs={{0,6},{2,0},{4,2},{6,4},{1,7},{3,1},{5,3},{7,5},{8,14},{10,8},{12,... | collective-permute-start | bytes 1572872 | tf_op jit(solution)/shard_map/ppermute | solution.py:34
  115.2 5.5 %collective-permute-done.12 = bf16[256,1024]{1,0:T(8,128)(2,1)} collective-permute-done((bf16[256,1024]{1,0:T(8,128)(2,1)S(1)}, bf16[256,1024]{1,0:T(8,128)(2,1)}, u32[]{:S(2)}, u32[]{:S(2)}) %collective-permute-start.12) | collective-permute-done | bytes 524320 | tf_op jit(solution)/shard_map/ppermute | solution.py:34
  120.7 10.9 %collective-permute-done.11 = bf16[256,1024]{1,0:T(8,128)(2,1)} collective-permute-done((bf16[256,1024]{1,0:T(8,128)(2,1)S(1)}, bf16[256,1024]{1,0:T(8,128)(2,1)}, u32[]{:S(2)}, u32[]{:S(2)}) %collective-permute-start.11) | collective-permute-done | bytes 524320 | tf_op jit(solution)/shard_map/ppermute | solution.py:34
  131.5 4.0 %collective-permute-done.10 = bf16[256,1024]{1,0:T(8,128)(2,1)} collective-permute-done((bf16[256,1024]{1,0:T(8,128)(2,1)S(1)}, bf16[256,1024]{1,0:T(8,128)(2,1)}, u32[]{:S(2)}, u32[]{:S(2)}) %collective-permute-start.10) | collective-permute-done | bytes 524320 | tf_op jit(solution)/shard_map/ppermute | solution.py:34
  135.5 2.1 %convolution_convert_fusion.2 = bf16[4,256,128]{2,1,0:T(8,128)(2,1)S(1)} fusion(bf16[1,256,1024]{2,1,0:T(8,128)(2,1)} %bitcast.18, bf16[1,256,1024]{2,1,0:T(8,128)(2,1)} %bitcast.17, bf16[1,256,1024]{2,1,0:T(8,128)(2,1)} %bitcast.16, bf16[1,256,1024]{2,1,0:T(8,128)(2,1)S(1)} %bitcast.83, bf16[2,128,1024]{2,1,0:T(8,128)(2,1)S(1)} %bitcast.85, s32[]{:T(128)S(6)} %select_n.59), kind=kOutput, calls=%fused_computation.3 | convolution fusion | flops 271712256 | bytes 2621444 | tf_op jit(solution)/shard_map/tmk,nk->tmn/dot_general | solution.py:168
  137.6 3.6 %collective-permute-start.13 = (bf16[4,256,128]{2,1,0:T(8,128)(2,1)S(1)}, bf16[4,256,128]{2,1,0:T(8,128)(2,1)S(1)}, u32[]{:S(2)}, u32[]{:S(2)}) collective-permute-start(bf16[4,256,128]{2,1,0:T(8,128)(2,1)S(1)} %convolution_convert_fusion.2), channel_id=1, source_target_pairs={{0,1},{1,0},{2,3},{3,2},{4,5},{5,4},{6,7},{7,6},{8,9},{9,8},{10,11... | collective-permute-start | bytes 786440 | tf_op jit(solution)/shard_map/ppermute | solution.py:34
  141.2 2.1 %fusion = f32[4,256,128]{2,1,0:T(8,128)S(1)} fusion(bf16[1,256,1024]{2,1,0:T(8,128)(2,1)} %bitcast.18, bf16[1,256,1024]{2,1,0:T(8,128)(2,1)} %bitcast.17, bf16[1,256,1024]{2,1,0:T(8,128)(2,1)} %bitcast.16, bf16[1,256,1024]{2,1,0:T(8,128)(2,1)S(1)} %bitcast.84, bf16[2,128,1024]{2,1,0:T(8,128)(2,1)S(1)} %bitcast.86, s32[]{:T(128)S(6)} %select_n.58), kind=kOutput, calls=%fused_computation.7 | convolution fusion | flops 271581184 | bytes 2883588 | tf_op jit(solution)/shard_map/tmk,nk->tmn/dot_general | solution.py:168
  144.1 6.7 %all-to-all-start.1 = ((bf16[16,64,128]{2,1,0:T(8,128)(2,1)}), bf16[16,64,128]{2,1,0:T(8,128)(2,1)S(1)}, u32[]{:S(2)}, u32[]{:S(2)}) async-start(bf16[16,64,128]{2,1,0:T(8,128)(2,1)} %bitcast.24), calls=%async_computation.1 | async-start | bytes 524288 | tf_op jit(solution)/shard_map/all_to_all | solution.py:25
  151.4 2.2 %collective-permute-start.14 = (f32[64,128]{1,0:T(8,128)S(1)}, f32[64,128]{1,0:T(8,128)S(1)}, u32[]{:S(2)}, u32[]{:S(2)}) collective-permute-start(f32[64,128]{1,0:T(8,128)S(1)} %reshape.76), channel_id=1, source_target_pairs={{0,1},{1,0},{2,3},{3,2},{4,5},{5,4},{6,7},{7,6},{8,9},{9,8},{10,11... | collective-permute-start | bytes 98312 | tf_op jit(solution)/shard_map/ppermute | solution.py:190
  154.5 2.8 %collective-permute-start.15 = (f32[64,128]{1,0:T(8,128)S(1)}, f32[64,128]{1,0:T(8,128)S(1)}, u32[]{:S(2)}, u32[]{:S(2)}) collective-permute-start(f32[64,128]{1,0:T(8,128)S(1)} %add.190), channel_id=1, source_target_pairs={{0,2},{2,0},{4,6},{6,4},{1,3},{3,1},{5,7},{7,5},{8,10},{10,8},{12,... | collective-permute-start | bytes 98312 | tf_op jit(solution)/shard_map/ppermute | solution.py:190
  157.3 2.2 %collective-permute-done.15 = f32[64,128]{1,0:T(8,128)S(1)} collective-permute-done((f32[64,128]{1,0:T(8,128)S(1)}, f32[64,128]{1,0:T(8,128)S(1)}, u32[]{:S(2)}, u32[]{:S(2)}) %collective-permute-start.15) | collective-permute-done | bytes 32800 | tf_op jit(solution)/shard_map/ppermute | solution.py:190
  159.4 4.0 %collective-permute-start.16 = (f32[64,128]{1,0:T(8,128)S(1)}, f32[64,128]{1,0:T(8,128)S(1)}, u32[]{:S(2)}, u32[]{:S(2)}) collective-permute-start(f32[64,128]{1,0:T(8,128)S(1)} %add.191), channel_id=1, source_target_pairs={{0,4},{2,6},{4,0},{6,2},{1,5},{3,7},{5,1},{7,3},{8,12},{10,14},{12... | collective-permute-start | bytes 98312 | tf_op jit(solution)/shard_map/ppermute | solution.py:190
  163.4 2.2 %collective-permute-done.16 = f32[64,128]{1,0:T(8,128)S(1)} collective-permute-done((f32[64,128]{1,0:T(8,128)S(1)}, f32[64,128]{1,0:T(8,128)S(1)}, u32[]{:S(2)}, u32[]{:S(2)}) %collective-permute-start.16) | collective-permute-done | bytes 32800 | tf_op jit(solution)/shard_map/ppermute | solution.py:190
  (53 shorter events, 14.3 us)
Async XLA Ops:
  0.6 1.2 copy-start
  3.3 12.3 %collective-permute-start.2 = (bf16[16,64,128]{2,1,0:T(8,128)(2,1)S(1)}, bf16[16,64,128]{2,1,0:T(8,128)(2,1)S(1)}, u32[]{:S(2)}, u32[]{:S(2)}) collective-permute-start(bf16[16,64,128]{2,1,0:T(8,128)(2,1)S(1)} %bitcast.71), channel_id=1, source_target_pairs={{0,128},{128,256},{256,384},{384,0},{1,129},{129,257},{257,385},{3... | collective-permute-start | bytes 786440 | tf_op jit(solution)/shard_map/ppermute | solution.py:34
  7.3 13.3 %collective-permute-start.1 = (bf16[16,64,128]{2,1,0:T(8,128)(2,1)S(1)}, bf16[16,64,128]{2,1,0:T(8,128)(2,1)S(1)}, u32[]{:S(2)}, u32[]{:S(2)}) collective-permute-start(bf16[16,64,128]{2,1,0:T(8,128)(2,1)S(1)} %bitcast.72), channel_id=1, source_target_pairs={{0,256},{128,384},{256,0},{384,128},{1,257},{129,385},{257,1},{385... | collective-permute-start | bytes 786440 | tf_op jit(solution)/shard_map/ppermute | solution.py:34
  11.8 8.7 %collective-permute-start = (bf16[16,64,128]{2,1,0:T(8,128)(2,1)S(1)}, bf16[16,64,128]{2,1,0:T(8,128)(2,1)S(1)}, u32[]{:S(2)}, u32[]{:S(2)}) collective-permute-start(bf16[16,64,128]{2,1,0:T(8,128)(2,1)S(1)} %bitcast.73), channel_id=1, source_target_pairs={{0,384},{128,0},{256,128},{384,256},{1,385},{129,1},{257,129},{385... | collective-permute-start | bytes 786440 | tf_op jit(solution)/shard_map/ppermute | solution.py:34
  20.6 3.1 %copy-start.1 = (bf16[16,64,128]{2,1,0:T(8,128)(2,1)}, bf16[16,64,128]{2,1,0:T(8,128)(2,1)S(1)}, u32[]{:S(2)}) copy-start(bf16[16,64,128]{2,1,0:T(8,128)(2,1)S(1)} %collective-permute-done.refs_1_) | copy-start | bytes 786436
  23.7 10.8 %collective-permute-start.3 = (bf16[256,1024]{1,0:T(8,128)(2,1)S(1)}, bf16[256,1024]{1,0:T(8,128)(2,1)}, u32[]{:S(2)}, u32[]{:S(2)}) collective-permute-start(bf16[256,1024]{1,0:T(8,128)(2,1)S(1)} %sketch.3), channel_id=1, source_target_pairs={{0,1},{1,0},{2,3},{3,2},{4,5},{5,4},{6,7},{7,6},{8,9},{9,8},{10,11... | collective-permute-start | bytes 1572872 | tf_op jit(solution)/shard_map/ppermute | solution.py:34
  30.4 1.0 copy-start.2
  35.6 8.8 %collective-permute-start.4 = (bf16[64,1024]{1,0:T(8,128)(2,1)S(1)}, bf16[64,1024]{1,0:T(8,128)(2,1)S(1)}, u32[]{:S(2)}, u32[]{:S(2)}) collective-permute-start(bf16[64,1024]{1,0:T(8,128)(2,1)S(1)} %get-tuple-element.4), channel_id=1, source_target_pairs={{0,2},{2,4},{4,6},{6,0},{1,3},{3,5},{5,7},{7,1},{8,10},{10,12},{12... | collective-permute-start | bytes 393224 | tf_op jit(solution)/shard_map/ppermute | solution.py:34
  37.6 7.1 %collective-permute-start.6 = (bf16[64,1024]{1,0:T(8,128)(2,1)S(1)}, bf16[64,1024]{1,0:T(8,128)(2,1)S(1)}, u32[]{:S(2)}, u32[]{:S(2)}) collective-permute-start(bf16[64,1024]{1,0:T(8,128)(2,1)S(1)} %get-tuple-element.5), channel_id=1, source_target_pairs={{0,6},{2,0},{4,2},{6,4},{1,7},{3,1},{5,3},{7,5},{8,14},{10,8},{12,... | collective-permute-start | bytes 393224 | tf_op jit(solution)/shard_map/ppermute | solution.py:34
  42.1 7.9 %collective-permute-start.5 = (bf16[64,1024]{1,0:T(8,128)(2,1)S(1)}, bf16[64,1024]{1,0:T(8,128)(2,1)S(1)}, u32[]{:S(2)}, u32[]{:S(2)}) collective-permute-start(bf16[64,1024]{1,0:T(8,128)(2,1)S(1)} %get-tuple-element.6), channel_id=1, source_target_pairs={{0,4},{2,6},{4,0},{6,2},{1,5},{3,7},{5,1},{7,3},{8,12},{10,14},{12... | collective-permute-start | bytes 393224 | tf_op jit(solution)/shard_map/ppermute | solution.py:34
  51.1 14.5 %copy-start.4 = (s32[64,1]{0,1:T(1,128)S(1)}, s32[64,1]{0,1:T(1,128)}, u32[]{:S(2)}) copy-start(s32[64,1]{0,1:T(1,128)} %param.10) | copy-start | bytes 772
  51.1 14.7 %copy-start.3 = (bf16[64,64,128]{2,1,0:T(8,128)(2,1)S(1)}, bf16[64,64,128]{2,1,0:T(8,128)(2,1)}, u32[]{:S(2)}) copy-start(bf16[64,64,128]{2,1,0:T(8,128)(2,1)} %param.9) | copy-start | bytes 3145732
  51.9 35.6 %all-to-all-start = ((bf16[4,64,1024]{2,1,0:T(8,128)(2,1)}), bf16[4,64,1024]{2,1,0:T(8,128)(2,1)S(1)}, u32[]{:S(2)}, u32[]{:S(2)}) async-start(bf16[4,64,1024]{2,1,0:T(8,128)(2,1)} %broadcast_in_dim.24), calls=%async_computation | async-start | bytes 1048576 | tf_op jit(solution)/shard_map/all_to_all | solution.py:25
  67.1 38.6 %collective-permute-start.7 = (bf16[64,1024]{1,0:T(8,128)(2,1)S(1)}, bf16[64,1024]{1,0:T(8,128)(2,1)S(1)}, u32[]{:S(2)}, u32[]{:S(2)}) collective-permute-start(bf16[64,1024]{1,0:T(8,128)(2,1)S(1)} %get-tuple-element.3), channel_id=1, source_target_pairs={{0,24},{8,0},{16,8},{24,16},{1,25},{9,1},{17,9},{25,17},{2,26},{10... | collective-permute-start | bytes 393224 | tf_op jit(solution)/shard_map/ppermute | solution.py:34
  72.1 33.7 %collective-permute-start.9 = (bf16[64,1024]{1,0:T(8,128)(2,1)S(1)}, bf16[64,1024]{1,0:T(8,128)(2,1)S(1)}, u32[]{:S(2)}, u32[]{:S(2)}) collective-permute-start(bf16[64,1024]{1,0:T(8,128)(2,1)S(1)} %get-tuple-element.3), channel_id=1, source_target_pairs={{0,8},{8,16},{16,24},{24,0},{1,9},{9,17},{17,25},{25,1},{2,10},{10... | collective-permute-start | bytes 393224 | tf_op jit(solution)/shard_map/ppermute | solution.py:34
  74.0 31.7 %collective-permute-start.8 = (bf16[64,1024]{1,0:T(8,128)(2,1)S(1)}, bf16[64,1024]{1,0:T(8,128)(2,1)S(1)}, u32[]{:S(2)}, u32[]{:S(2)}) collective-permute-start(bf16[64,1024]{1,0:T(8,128)(2,1)S(1)} %get-tuple-element.3), channel_id=1, source_target_pairs={{0,16},{8,24},{16,0},{24,8},{1,17},{9,25},{17,1},{25,9},{2,18},{10... | collective-permute-start | bytes 393224 | tf_op jit(solution)/shard_map/ppermute | solution.py:34
  87.5 56.6 %all-to-all-start.2 = ((bf16[64,2,2048]{2,1,0:T(2,128)(2,1)}), bf16[64,2,2048]{2,1,0:T(2,128)(2,1)S(1)}, u32[]{:S(2)}, u32[]{:S(2)}) async-start(bf16[64,2,2048]{2,1,0:T(2,128)(2,1)} %reshape.73), calls=%async_computation.2 | async-start | bytes 1048576 | tf_op jit(solution)/shard_map/all_to_all | solution.py:25
  105.8 14.8 %collective-permute-start.12 = (bf16[256,1024]{1,0:T(8,128)(2,1)S(1)}, bf16[256,1024]{1,0:T(8,128)(2,1)}, u32[]{:S(2)}, u32[]{:S(2)}) collective-permute-start(bf16[256,1024]{1,0:T(8,128)(2,1)S(1)} %bitcast.80), channel_id=1, source_target_pairs={{0,2},{2,4},{4,6},{6,0},{1,3},{3,5},{5,7},{7,1},{8,10},{10,12},{12... | collective-permute-start | bytes 1572872 | tf_op jit(solution)/shard_map/ppermute | solution.py:34
  107.8 23.7 %collective-permute-start.11 = (bf16[256,1024]{1,0:T(8,128)(2,1)S(1)}, bf16[256,1024]{1,0:T(8,128)(2,1)}, u32[]{:S(2)}, u32[]{:S(2)}) collective-permute-start(bf16[256,1024]{1,0:T(8,128)(2,1)S(1)} %bitcast.81), channel_id=1, source_target_pairs={{0,4},{2,6},{4,0},{6,2},{1,5},{3,7},{5,1},{7,3},{8,12},{10,14},{12... | collective-permute-start | bytes 1572872 | tf_op jit(solution)/shard_map/ppermute | solution.py:34
  112.1 23.4 %collective-permute-start.10 = (bf16[256,1024]{1,0:T(8,128)(2,1)S(1)}, bf16[256,1024]{1,0:T(8,128)(2,1)}, u32[]{:S(2)}, u32[]{:S(2)}) collective-permute-start(bf16[256,1024]{1,0:T(8,128)(2,1)S(1)} %bitcast.82), channel_id=1, source_target_pairs={{0,6},{2,0},{4,2},{6,4},{1,7},{3,1},{5,3},{7,5},{8,14},{10,8},{12,... | collective-permute-start | bytes 1572872 | tf_op jit(solution)/shard_map/ppermute | solution.py:34
  137.6 5.7 %collective-permute-start.13 = (bf16[4,256,128]{2,1,0:T(8,128)(2,1)S(1)}, bf16[4,256,128]{2,1,0:T(8,128)(2,1)S(1)}, u32[]{:S(2)}, u32[]{:S(2)}) collective-permute-start(bf16[4,256,128]{2,1,0:T(8,128)(2,1)S(1)} %convolution_convert_fusion.2), channel_id=1, source_target_pairs={{0,1},{1,0},{2,3},{3,2},{4,5},{5,4},{6,7},{7,6},{8,9},{9,8},{10,11... | collective-permute-start | bytes 786440 | tf_op jit(solution)/shard_map/ppermute | solution.py:34
  144.1 22.2 %all-to-all-start.1 = ((bf16[16,64,128]{2,1,0:T(8,128)(2,1)}), bf16[16,64,128]{2,1,0:T(8,128)(2,1)S(1)}, u32[]{:S(2)}, u32[]{:S(2)}) async-start(bf16[16,64,128]{2,1,0:T(8,128)(2,1)} %bitcast.24), calls=%async_computation.1 | async-start | bytes 524288 | tf_op jit(solution)/shard_map/all_to_all | solution.py:25
  151.4 3.1 %collective-permute-start.14 = (f32[64,128]{1,0:T(8,128)S(1)}, f32[64,128]{1,0:T(8,128)S(1)}, u32[]{:S(2)}, u32[]{:S(2)}) collective-permute-start(f32[64,128]{1,0:T(8,128)S(1)} %reshape.76), channel_id=1, source_target_pairs={{0,1},{1,0},{2,3},{3,2},{4,5},{5,4},{6,7},{7,6},{8,9},{9,8},{10,11... | collective-permute-start | bytes 98312 | tf_op jit(solution)/shard_map/ppermute | solution.py:190
  154.5 4.9 %collective-permute-start.15 = (f32[64,128]{1,0:T(8,128)S(1)}, f32[64,128]{1,0:T(8,128)S(1)}, u32[]{:S(2)}, u32[]{:S(2)}) collective-permute-start(f32[64,128]{1,0:T(8,128)S(1)} %add.190), channel_id=1, source_target_pairs={{0,2},{2,0},{4,6},{6,4},{1,3},{3,1},{5,7},{7,5},{8,10},{10,8},{12,... | collective-permute-start | bytes 98312 | tf_op jit(solution)/shard_map/ppermute | solution.py:190
  159.4 6.2 %collective-permute-start.16 = (f32[64,128]{1,0:T(8,128)S(1)}, f32[64,128]{1,0:T(8,128)S(1)}, u32[]{:S(2)}, u32[]{:S(2)}) collective-permute-start(f32[64,128]{1,0:T(8,128)S(1)} %add.191), channel_id=1, source_target_pairs={{0,4},{2,6},{4,0},{6,2},{1,5},{3,7},{5,1},{7,3},{8,12},{10,14},{12... | collective-permute-start | bytes 98312 | tf_op jit(solution)/shard_map/ppermute | solution.py:190
